TPU v7x, 128 devices: a whole 4x4x4 slice. The times are simulated.
128 devices in a mesh: rep: 16 (over x, z), grp: 8 (over y, core).
Axes of the slice: x: 4, y: 4, z: 4, core: 2. Of those that a mesh axis runs over, the one named last changes fastest.
Arguments:
- inputs: bfloat16 [2, 262144, 1152], P(None, ('rep', 'grp')), may hold values from -6 to 6
- out_grads: bfloat16 [2, 262144, 1152], P(None, ('rep', 'grp')), may hold values from -6 to 6
- weights: bfloat16 [2, 1152, 1152], P(None, 'grp'), may hold values from -3 to 3
- biases: bfloat16 [2, 1152], P(None, 'grp'), may hold values from -3 to 3
- errors: float32 [16, 2, 1152, 1152], P('rep', None, 'grp'), may hold values from -6 to 6
- momenta: float32 [2, 1152, 1152], P(None, 'grp'), may hold values from -3 to 3
- bias_momenta: float32 [2, 1152], P(None, 'grp'), may hold values from -3 to 3
- q_start: float32 [2, 1152, 32], replicated, may hold values from -6 to 6
Outputs:
- new_weights: bfloat16 [2, 1152, 1152], replicated
- new_biases: bfloat16 [2, 1152], replicated
- new_errors: float32 [16, 2, 1152, 1152], P('rep', None, 'grp')
- new_momenta: float32 [2, 1152, 1152], P(None, 'grp')
- new_bias_momenta: float32 [2, 1152], P(None, 'grp')
All inputs are finite; a program needn't handle non-finite values.
Results may differ from a plain program's by a relative error of at most 0.0045.
Values may be sent and summed in bfloat16 or wider, within the bound.
No kernel may reach another device: no remote copies, remote signals or barrier semaphores. Data moves between devices by JAX's collectives and lax.ppermute only.
A program may use at most 256 MiB of HBM per device.

v0:
```python
import functools

import jax
import jax.numpy as jnp
from jax import lax
from jax.experimental import pallas as pl
from jax.experimental.pallas import tpu as pltpu
from jax.sharding import Mesh
from jax.sharding import PartitionSpec as P


ROUNDS = 2
NS_STEPS = 5
HIGH = lax.Precision.HIGHEST
BF = jnp.bfloat16
F32 = jnp.float32


def ring(count, step):
    return [(i, (i + step) % count) for i in range(count)]


def pick(stack, index, axis=0):
    return lax.dynamic_index_in_dim(stack, index, axis, keepdims=False)


def hi_lo(row):
    high = row.astype(BF)
    low = (row - high.astype(F32)).astype(BF)
    return jnp.concatenate([high[None], low[None], jnp.zeros((6, row.shape[0]), BF)], 0)


def from_hi_lo(rows):
    return rows[0].astype(F32) + rows[1].astype(F32)


def paired(parts):
    return (parts[0] + parts[2]) + (parts[1] + parts[3])


def split3(value):
    one = value.astype(BF)
    rest = value - one.astype(F32)
    two = rest.astype(BF)
    three = (rest - two.astype(F32)).astype(BF)
    return jnp.concatenate([one, two, three], 0)


def by_three(left, right, dims):
    rank = left.shape[0]
    out = lax.dot_general(split3(left), right, dims, preferred_element_type=F32)
    return out[:rank] + out[rank : 2 * rank] + out[2 * rank :]


def inverse_root(gram):
    fro = jnp.sqrt(jnp.sum(gram * gram)) + 1e-06
    eye = jnp.eye(gram.shape[-1], dtype=F32)
    ymat = gram / fro
    zmat = eye
    for _ in range(NS_STEPS):
        tmat = 1.5 * eye - 0.5 * jnp.dot(zmat, ymat, precision=HIGH)
        ymat = jnp.dot(ymat, tmat, precision=HIGH)
        zmat = jnp.dot(tmat, zmat, precision=HIGH)
    return zmat, jnp.sqrt(fro)


def products(left, right):
    l1 = left.astype(BF)
    rest = left - l1.astype(F32)
    l2 = rest.astype(BF)
    l3 = (rest - l2.astype(F32)).astype(BF)
    r1 = right.astype(BF)
    rest = right - r1.astype(F32)
    r2 = rest.astype(BF)
    r3 = (rest - r2.astype(F32)).astype(BF)
    return (
        jnp.concatenate([l1, l1, l2, l1, l2, l3], -2),
        jnp.concatenate([r1, r2, r1, r3, r2, r1], -2),
    )


def final_kernel(reps, ys, place_ref, *refs):
    mine, theirs = refs[0:2], refs[2:4]
    left, right = refs[4:6], refs[6]
    merged_ref, momenta_ref, out_ref, errors_ref, new_momenta_ref = refs[7:]
    rows = out_ref.shape[1]
    step = pl.program_id(0)
    for layer in range(out_ref.shape[0]):
        approx = lax.dot_general(
            left[layer][...],
            right[layer],
            (((0,), (0,)), ((), ())),
            preferred_element_type=F32,
        )[:rows] * (1.0 / reps)

        @pl.when(step < ys)
        def _():
            out_ref[layer] = (mine[layer][0, :rows].astype(F32) - 0.5 * approx).astype(BF)

        @pl.when(step >= ys)
        def _():
            out_ref[layer] = (theirs[layer][0, :rows].astype(F32) - 0.5 * approx).astype(BF)

        @pl.when(step == 0)
        def _():
            errors_ref[layer] = merged_ref[layer] - approx
            new_momenta_ref[layer] = 0.9 * momenta_ref[layer] + approx


def finish(mine, theirs, left, right, merged, momenta, place, reps):
    ys, held, width = mine[0].shape
    rows = merged.shape[1]
    layers, deep, _ = right.shape
    old = lambda spot: pl.BlockSpec((1, held, width), spot)
    whole = lambda *shape: pl.BlockSpec(shape, lambda i, place: (0,) * len(shape))
    return pl.pallas_call(
        functools.partial(final_kernel, reps, ys),
        out_shape=(
            jax.ShapeDtypeStruct((layers, 2 * ys * rows, width), BF),
            jax.ShapeDtypeStruct((layers, rows, width), F32),
            jax.ShapeDtypeStruct((layers, rows, width), F32),
        ),
        grid_spec=pltpu.PrefetchScalarGridSpec(
            num_scalar_prefetch=1,
            grid=(2 * ys,),
            in_specs=[old(lambda i, place: (jnp.minimum(i, ys - 1), 0, 0))] * layers
            + [old(lambda i, place: (jnp.maximum(i - ys, 0), 0, 0))] * layers
            + [
                pl.BlockSpec((deep, 256), lambda i, place: (0, place[2 * ys + i])),
                pl.BlockSpec((deep, 256), lambda i, place: (0, place[4 * ys + i])),
                whole(layers, deep, width),
                whole(layers, rows, width),
                whole(layers, rows, width),
            ],
            out_specs=[
                pl.BlockSpec((layers, rows, width), lambda i, place: (0, place[i], 0)),
                whole(layers, rows, width),
                whole(layers, rows, width),
            ],
        ),
        name="finish",
    )(place, *mine, *theirs, *left, right, merged, momenta)


def body(inputs, out_grads, weights, biases, errors, momenta, bias_momenta, q_start):
    layers, tok, width = inputs.shape
    cores = lax.axis_size("core")
    ys = lax.axis_size("y")
    xs = lax.axis_size("x")
    reps = xs * lax.axis_size("z")
    rows = width // (cores * ys)
    rank = q_start.shape[-1]
    scale = float(tok) ** (-0.5)
    core, ypos, xpos = lax.axis_index("core"), lax.axis_index("y"), lax.axis_index("x")

    def swap(value):
        return lax.ppermute(value, "core", ring(cores, 1))

    def from_back(value, axis, step):
        return lax.ppermute(value, axis, ring(4, step))

    def everyone(value, axis):
        return [value] + [from_back(value, axis, k) for k in (1, 2, 3)]

    def natural(parts, position):
        ordered = []
        for j in range(4):
            value = parts[-j % 4]
            for spot in (1, 2, 3):
                value = jnp.where(position == spot, parts[(spot - j) % 4], value)
            ordered.append(value)
        return ordered

    def old_of(layer, after=None):
        w, m = weights[layer], momenta[layer]
        if after is not None:
            w, m, _ = lax.optimization_barrier((w, m, after))
        shard = (w.astype(F32) - 0.45 * m).astype(BF)
        row = biases[layer].astype(F32) - 0.45 * bias_momenta[layer]
        shard = jnp.concatenate([shard, hi_lo(jnp.pad(row, (0, width - rows)))], 0)
        parts = everyone(shard, "y")
        mine = jnp.stack(parts)
        theirs = swap(mine)
        return mine, theirs

    mine0, theirs0 = old_of(0)

    def chip_blocks(layer, after=None):
        x, y = inputs, out_grads
        if after is not None:
            x, y, _ = lax.optimization_barrier((x, y, after))
        part = jnp.einsum("tr,te->re", x[layer], y[layer], preferred_element_type=F32)
        part = lax.optimization_barrier(part).reshape(ys * cores, rows, width)
        got = swap(
            pick(part.reshape(ys, cores, rows, width), 1 - core, 1).astype(BF)
        )
        blocks = []
        for k in range(4):
            there = (ypos + k) % 4
            blocks.append(pick(part, there * cores + core) + pick(got, there).astype(F32))
        return blocks[0], [b.astype(BF) for b in blocks[1:]]

    def merge(layer, own, blocks):
        for k in (1, 3, 2):
            block = from_back(blocks[k - 1], "y", k)
            own = own + block.astype(F32)
        return own * scale + errors[0, layer]

    own0, blocks0 = chip_blocks(0)
    own1, blocks1 = chip_blocks(1, blocks0)
    merged = jnp.stack([merge(0, own0, blocks0), merge(1, own1, blocks1)])
    col_sums = jnp.sum(out_grads, axis=1, dtype=F32)

    got = swap(
        jnp.concatenate([pick(merged, 1 - core).astype(BF), hi_lo(pick(col_sums, 1 - core))], 0)
    )
    mine1, theirs1 = old_of(1)
    both = jnp.stack([pick(merged, core), got[:rows].astype(F32)]).reshape(4, rows // 2, width)
    bias = pick(col_sums, core) + from_hi_lo(got[rows:])
    bias_rows = hi_lo(bias)
    half = rows // 2

    def loaded(main):
        return jnp.concatenate([main.astype(BF), bias_rows], 0)

    parts = [loaded(pick(both, xpos))]
    for k in (1, 2, 3):
        block = loaded(pick(both, (xpos + k) % 4))
        parts.append(from_back(block, "x", k))
    main = paired([p[:half].astype(F32) for p in parts])
    bias = paired([from_hi_lo(p[half:]) for p in parts])
    bias_rows = hi_lo(bias)
    parts = everyone(loaded(main), "z")
    main = paired([p[:half].astype(F32) for p in parts]).astype(BF)
    bias = paired([from_hi_lo(p[half:]) for p in parts])
    parts = everyone(main, "x")
    quarter = natural(parts, xpos)
    gap = jnp.zeros((256 - rows, width), BF)
    total = jnp.concatenate(quarter[:2] + [gap] + quarter[2:] + [gap], 0)

    q = pick(q_start, core).T
    for rnd in range(ROUNDS):
        p = by_three(q, total, (((1,), (1,)), ((), ())))
        gram = lax.dot_general(p, p, (((1,), (1,)), ((), ())), precision=HIGH)
        u = by_three(p, total, (((1,), (0,)), ((), ())))
        packed = jnp.concatenate([u, jnp.pad(gram, ((0, 0), (0, 128 - rank)))], 1)
        if rnd == 0:
            last = jnp.concatenate([bias[None], jnp.zeros((1, 128), F32)], 1)
            packed = jnp.concatenate([packed, jnp.pad(last, ((0, 7), (0, 0)))], 0)
        else:
            packed = jnp.concatenate([packed, p], 1)
        parts = everyone(packed, "y")
        summed = paired([part[:, : width + 128] for part in parts])
        zmat, root = inverse_root(summed[:rank, width : width + rank])
        q = lax.dot_general(zmat, summed[:rank, :width], (((0,), (0,)), ((), ())), precision=HIGH) / root
        if rnd == 0:
            bias = summed[rank, :width]
    p_all = jnp.concatenate(natural([part[:, width + 128 :] for part in parts], ypos), 1)
    phat = lax.dot_general(zmat, p_all, (((0,), (0,)), ((), ())), precision=HIGH) / root

    last = jnp.concatenate([bias[None], jnp.zeros((1, phat.shape[1]), F32)], 1)
    packed = jnp.concatenate(
        [jnp.concatenate([q, phat], 1), jnp.pad(last, ((0, 7), (0, 0)))], 0
    )
    other = swap(packed)
    pair = [jnp.where(core == layer, packed, other) for layer in range(layers)]
    bias = jnp.stack([p[rank, :width] for p in pair])
    factors = [products(p[:rank, width:], p[:rank, :width]) for p in pair]

    grp = ypos * cores + core
    i = jnp.arange(ys * cores)
    back, side = i % ys, core ^ (i // ys)
    where = ((ypos - back) % 4) * cores
    place = jnp.concatenate([where + side, where + side, where + (side ^ 1)]).astype(jnp.int32)
    new_weights, new_errors, new_momenta = finish(
        [mine0, mine1],
        [theirs0, theirs1],
        [f[0] for f in factors],
        jnp.stack([f[1] for f in factors]),
        merged,
        momenta,
        place,
        reps,
    )

    bias_grad = bias * (scale / reps)
    new_bias_momenta = 0.9 * bias_momenta + lax.dynamic_slice_in_dim(bias_grad, grp * rows, rows, 1)
    b_all = []
    for mine, theirs in ((mine0, theirs0), (mine1, theirs1)):
        both = []
        for stack in (mine, theirs):
            pieces = stack[:, rows : rows + 2, :rows].astype(F32)
            both.append(jnp.stack(natural(list(pieces[:, 0] + pieces[:, 1]), ypos)))
        even = jnp.where(core == 0, both[0], both[1])
        odd = jnp.where(core == 0, both[1], both[0])
        b_all.append(jnp.stack([even, odd], 1).reshape(width))
    b_all = jnp.stack(b_all)
    new_biases = (b_all - 0.5 * bias_grad).astype(BF)
    return (new_weights, new_biases, new_errors[None], new_momenta, new_bias_momenta)


def solution(mesh):
    split = Mesh(mesh.devices.reshape(4, 4, 4, 2), ("x", "z", "y", "core"))
    rep, grp = ("x", "z"), ("y", "core")
    placed = (
        P(None, rep + grp, None),
        P(None, rep + grp, None),
        P(None, grp, None),
        P(None, grp),
        P(rep, None, grp, None),
        P(None, grp, None),
        P(None, grp),
        P(),
    )

    return jax.shard_map(
        body,
        mesh=split,
        in_specs=placed,
        out_specs=(P(), P(), P(rep, None, grp, None), P(None, grp, None), P(None, grp)),
        check_vma=False,
    )
```

profile of v0, /device:TPU:1, one launch (start us, length us, event | category | flops | bytes accessed | tf_op | source)
XLA Modules:
  0.0 183.9 jit_solution(18052780260657186905)
XLA Ops:
  1.4 1.6 fusion.34
  3.9 2.1 %collective-permute-start = (bf16[152,1152]{1,0:T(8,128)(2,1)}, bf16[152,1152]{1,0:T(8,128)(2,1)}, u32[]{:S(2)}, u32[]{:S(2)}) collective-permute-start(bf16[152,1152]{1,0:T(8,128)(2,1)} %get-tuple-element.72), channel_id=1, source_target_pairs={{0,2},{2,4},{4,6},{6,0},{1,3},{3,5},{5,7},{7,1},{8,10},{10,12},{12... | collective-permute-start | bytes 1050632 | tf_op jit(solution)/shard_map/ppermute | solution.py:160
  6.0 2.6 %collective-permute-start.1 = (bf16[152,1152]{1,0:T(8,128)(2,1)}, bf16[152,1152]{1,0:T(8,128)(2,1)}, u32[]{:S(2)}, u32[]{:S(2)}) collective-permute-start(bf16[152,1152]{1,0:T(8,128)(2,1)} %get-tuple-element.72), channel_id=1, source_target_pairs={{0,4},{2,6},{4,0},{6,2},{1,5},{3,7},{5,1},{7,3},{8,12},{10,14},{12... | collective-permute-start | bytes 1050632 | tf_op jit(solution)/shard_map/ppermute | solution.py:160
  8.6 1.1 collective-permute-start.2
  9.7 12.5 %fusion.3 = f32[1152,1152]{1,0:T(8,128)} fusion(bf16[2,2048,1152]{2,1,0:T(8,128)(2,1)} %param.9, bf16[2,2048,1152]{2,1,0:T(8,128)(2,1)} %param.8), kind=kOutput, calls=%fused_computation.4 | convolution fusion | flops 5435817984 | bytes 14745600 | tf_op jit(solution)/shard_map/tr,te->re/dot_general | solution.py:192
  22.2 1.9 %fusion.10 = bf16[4,144,1152]{2,1,0:T(8,128)(2,1)S(1)} fusion(f32[4,2,144,1152]{3,2,1,0:T(8,128)} %bitcast.372, s32[]{:T(128)S(6)} %select_n.549), kind=kLoop, calls=%fused_computation.23 | loop fusion | bytes 2654212 | tf_op jit(solution)/shard_map/convert_element_type | solution.py:195
  24.1 1.6 collective-permute-start.8
  25.7 5.0 %convert_reduce_fusion = f32[2,1152]{1,0:T(2,128)S(1)} fusion(bf16[2,2048,1152]{2,1,0:T(8,128)(2,1)} %param.9), kind=kLoop, calls=%fused_computation | loop fusion | flops 9434880 | bytes 9446400 | tf_op jit(solution)/shard_map/reduce_sum | solution.py:212
  31.5 1.4 pad_maximum_fusion.1.refs_0_
  33.2 1.9 %fusion.36 = (bf16[144,1152]{1,0:T(8,128)(2,1)S(1)}, bf16[144,1152]{1,0:T(8,128)(2,1)S(1)}, bf16[144,1152]{1,0:T(8,128)(2,1)S(1)}) fusion(f32[8,144,1152]{2,1,0:T(8,128)} %bitcast.373, s32[]{:T(128)S(6)} %select_n.555, bf16[4,144,1152]{2,1,0:T(8,128)(2,1)S(1)} %collective-permute-done.8, s32[]{:T(128)S(6)} %select_n.556, s32[]{:T(128)S(6)} %select_n.559, ...), kind=kLoop, calls=%fused_computation.82 | loop fusion | flops 1492992 | bytes 3981336 | tf_op jit(solution)/shard_map/convert_element_type | solution.py:201
  35.2 10.1 %fusion = f32[1152,1152]{1,0:T(8,128)S(1)} fusion(bf16[2,2048,1152]{2,1,0:T(8,128)(2,1)} %param.9, bf16[2,2048,1152]{2,1,0:T(8,128)(2,1)} %param.8), kind=kOutput, calls=%fused_computation.1 | convolution fusion | flops 5435817984 | bytes 14745600 | tf_op jit(solution)/shard_map/tr,te->re/dot_general | solution.py:192
  47.0 2.2 %collective-permute-start.11 = (bf16[144,1152]{1,0:T(8,128)(2,1)S(1)}, bf16[144,1152]{1,0:T(8,128)(2,1)S(1)}, u32[]{:S(2)}, u32[]{:S(2)}) collective-permute-start(bf16[144,1152]{1,0:T(8,128)(2,1)S(1)} %get-tuple-element.52), channel_id=1, source_target_pairs={{0,4},{2,6},{4,0},{6,2},{1,5},{3,7},{5,1},{7,3},{8,12},{10,14},{12... | collective-permute-start | bytes 995336 | tf_op jit(solution)/shard_map/ppermute | solution.py:160
  49.5 0.8 copy-done.2
  50.8 2.1 %collective-permute-start.14 = (bf16[144,1152]{1,0:T(8,128)(2,1)S(1)}, bf16[144,1152]{1,0:T(8,128)(2,1)S(1)}, u32[]{:S(2)}, u32[]{:S(2)}) collective-permute-start(bf16[144,1152]{1,0:T(8,128)(2,1)S(1)} %get-tuple-element.50), channel_id=1, source_target_pairs={{0,6},{2,0},{4,2},{6,4},{1,7},{3,1},{5,3},{7,5},{8,14},{10,8},{12,... | collective-permute-start | bytes 995336 | tf_op jit(solution)/shard_map/ppermute | solution.py:160
  53.0 3.1 %collective-permute-done.10 = bf16[144,1152]{1,0:T(8,128)(2,1)S(1)} collective-permute-done((bf16[144,1152]{1,0:T(8,128)(2,1)S(1)}, bf16[144,1152]{1,0:T(8,128)(2,1)S(1)}, u32[]{:S(2)}, u32[]{:S(2)}) %collective-permute-start.10) | collective-permute-done | bytes 331808 | tf_op jit(solution)/shard_map/ppermute | solution.py:160
  56.6 1.1 collective-permute-done.11
  57.7 7.7 %collective-permute-done.9 = bf16[144,1152]{1,0:T(8,128)(2,1)S(1)} collective-permute-done((bf16[144,1152]{1,0:T(8,128)(2,1)S(1)}, bf16[144,1152]{1,0:T(8,128)(2,1)S(1)}, u32[]{:S(2)}, u32[]{:S(2)}) %collective-permute-start.9) | collective-permute-done | bytes 331808 | tf_op jit(solution)/shard_map/ppermute | solution.py:160
  65.4 7.7 %collective-permute-done.13 = bf16[144,1152]{1,0:T(8,128)(2,1)S(1)} collective-permute-done((bf16[144,1152]{1,0:T(8,128)(2,1)S(1)}, bf16[144,1152]{1,0:T(8,128)(2,1)S(1)}, u32[]{:S(2)}, u32[]{:S(2)}) %collective-permute-start.13) | collective-permute-done | bytes 331808 | tf_op jit(solution)/shard_map/ppermute | solution.py:160
  73.1 5.9 %collective-permute-done.15 = bf16[144,1152]{1,0:T(8,128)(2,1)S(1)} collective-permute-done((bf16[144,1152]{1,0:T(8,128)(2,1)S(1)}, bf16[144,1152]{1,0:T(8,128)(2,1)S(1)}, u32[]{:S(2)}, u32[]{:S(2)}) %collective-permute-start.15) | collective-permute-done | bytes 331808 | tf_op jit(solution)/shard_map/ppermute | solution.py:160
  79.1 1.6 fusion.29
  81.0 1.2 collective-permute-start.16
  82.4 2.2 %collective-permute-start.4 = (bf16[152,1152]{1,0:T(8,128)(2,1)S(1)}, bf16[152,1152]{1,0:T(8,128)(2,1)S(1)}, u32[]{:S(2)}, u32[]{:S(2)}) collective-permute-start(bf16[152,1152]{1,0:T(8,128)(2,1)S(1)} %get-tuple-element.70), channel_id=1, source_target_pairs={{0,4},{2,6},{4,0},{6,2},{1,5},{3,7},{5,1},{7,3},{8,12},{10,14},{12... | collective-permute-start | bytes 1050632 | tf_op jit(solution)/shard_map/ppermute | solution.py:160
  84.6 0.8 fusion.158
  85.4 1.0 fusion.42
  86.6 2.8 %collective-permute-start.17 = (bf16[80,1152]{1,0:T(8,128)(2,1)S(1)}, bf16[80,1152]{1,0:T(8,128)(2,1)S(1)}, u32[]{:S(2)}, u32[]{:S(2)}) collective-permute-start(bf16[80,1152]{1,0:T(8,128)(2,1)S(1)} %get-tuple-element.80), channel_id=1, source_target_pairs={{0,64},{32,96},{64,0},{96,32},{1,65},{33,97},{65,1},{97,33},{2,66}... | collective-permute-start | bytes 552968 | tf_op jit(solution)/shard_map/ppermute | solution.py:160
  89.7 2.4 %collective-permute-start.19 = (bf16[80,1152]{1,0:T(8,128)(2,1)S(1)}, bf16[80,1152]{1,0:T(8,128)(2,1)S(1)}, u32[]{:S(2)}, u32[]{:S(2)}) collective-permute-start(bf16[80,1152]{1,0:T(8,128)(2,1)S(1)} %get-tuple-element.82), channel_id=1, source_target_pairs={{0,96},{32,0},{64,32},{96,64},{1,97},{33,1},{65,33},{97,65},{2,98}... | collective-permute-start | bytes 552968 | tf_op jit(solution)/shard_map/ppermute | solution.py:160
  92.1 1.2 pad_maximum_fusion.refs_7_
  93.3 0.8 collective-permute-done.17
  94.1 1.2 collective-permute-start.3
  95.3 3.4 %collective-permute-done.18 = bf16[80,1152]{1,0:T(8,128)(2,1)S(1)} collective-permute-done((bf16[80,1152]{1,0:T(8,128)(2,1)S(1)}, bf16[80,1152]{1,0:T(8,128)(2,1)S(1)}, u32[]{:S(2)}, u32[]{:S(2)}) %collective-permute-start.18) | collective-permute-done | bytes 184352 | tf_op jit(solution)/shard_map/ppermute | solution.py:160
  98.8 3.7 %collective-permute-start.20 = (bf16[80,1152]{1,0:T(8,128)(2,1)S(1)}, bf16[80,1152]{1,0:T(8,128)(2,1)S(1)}, u32[]{:S(2)}, u32[]{:S(2)}) collective-permute-start(bf16[80,1152]{1,0:T(8,128)(2,1)S(1)} %pad_maximum_fusion.8), channel_id=1, source_target_pairs={{0,16},{8,24},{16,0},{24,8},{1,17},{9,25},{17,1},{25,9},{2,18},{10... | collective-permute-start | bytes 552968 | tf_op jit(solution)/shard_map/ppermute | solution.py:160
  103.2 1.9 %collective-permute-start.22 = (bf16[80,1152]{1,0:T(8,128)(2,1)S(1)}, bf16[80,1152]{1,0:T(8,128)(2,1)S(1)}, u32[]{:S(2)}, u32[]{:S(2)}) collective-permute-start(bf16[80,1152]{1,0:T(8,128)(2,1)S(1)} %pad_maximum_fusion.8), channel_id=1, source_target_pairs={{0,24},{8,0},{16,8},{24,16},{1,25},{9,1},{17,9},{25,17},{2,26},{10... | collective-permute-start | bytes 552968 | tf_op jit(solution)/shard_map/ppermute | solution.py:160
  105.4 1.6 collective-permute-start.7
  107.0 4.2 %collective-permute-done.21 = bf16[80,1152]{1,0:T(8,128)(2,1)S(1)} collective-permute-done((bf16[80,1152]{1,0:T(8,128)(2,1)S(1)}, bf16[80,1152]{1,0:T(8,128)(2,1)S(1)}, u32[]{:S(2)}, u32[]{:S(2)}) %collective-permute-start.21) | collective-permute-done | bytes 184352 | tf_op jit(solution)/shard_map/ppermute | solution.py:160
  111.4 2.2 %collective-permute-start.23 = (bf16[72,1152]{1,0:T(8,128)(2,1)S(1)}, bf16[72,1152]{1,0:T(8,128)(2,1)S(1)}, u32[]{:S(2)}, u32[]{:S(2)}) collective-permute-start(bf16[72,1152]{1,0:T(8,128)(2,1)S(1)} %add_convert_fusion.6), channel_id=1, source_target_pairs={{0,96},{32,0},{64,32},{96,64},{1,97},{33,1},{65,33},{97,65},{2,98}... | collective-permute-start | bytes 497672 | tf_op jit(solution)/shard_map/ppermute | solution.py:160
  113.5 1.0 collective-permute-start.24
  114.6 2.6 %collective-permute-done.23 = bf16[72,1152]{1,0:T(8,128)(2,1)S(1)} collective-permute-done((bf16[72,1152]{1,0:T(8,128)(2,1)S(1)}, bf16[72,1152]{1,0:T(8,128)(2,1)S(1)}, u32[]{:S(2)}, u32[]{:S(2)}) %collective-permute-start.23) | collective-permute-done | bytes 165920 | tf_op jit(solution)/shard_map/ppermute | solution.py:160
  117.2 2.2 %collective-permute-done.24 = bf16[72,1152]{1,0:T(8,128)(2,1)S(1)} collective-permute-done((bf16[72,1152]{1,0:T(8,128)(2,1)S(1)}, bf16[72,1152]{1,0:T(8,128)(2,1)S(1)}, u32[]{:S(2)}, u32[]{:S(2)}) %collective-permute-start.24) | collective-permute-done | bytes 165920 | tf_op jit(solution)/shard_map/ppermute | solution.py:160
  119.3 4.5 %collective-permute-done.25 = bf16[72,1152]{1,0:T(8,128)(2,1)S(1)} collective-permute-done((bf16[72,1152]{1,0:T(8,128)(2,1)S(1)}, bf16[72,1152]{1,0:T(8,128)(2,1)S(1)}, u32[]{:S(2)}, u32[]{:S(2)}) %collective-permute-start.25) | collective-permute-done | bytes 165920 | tf_op jit(solution)/shard_map/ppermute | solution.py:160
  126.8 2.6 %collective-permute-start.28 = (f32[40,1280]{1,0:T(8,128)S(1)}, f32[40,1280]{1,0:T(8,128)S(1)}, u32[]{:S(2)}, u32[]{:S(2)}) collective-permute-start(f32[40,1280]{1,0:T(8,128)S(1)} %select_maximum_fusion.1), channel_id=1, source_target_pairs={{0,6},{2,0},{4,2},{6,4},{1,7},{3,1},{5,3},{7,5},{8,14},{10,8},{12,... | collective-permute-start | bytes 614408 | tf_op jit(solution)/shard_map/ppermute | solution.py:160
  129.4 3.4 %collective-permute-done.26 = f32[40,1280]{1,0:T(8,128)S(1)} collective-permute-done((f32[40,1280]{1,0:T(8,128)S(1)}, f32[40,1280]{1,0:T(8,128)S(1)}, u32[]{:S(2)}, u32[]{:S(2)}) %collective-permute-start.26) | collective-permute-done | bytes 204832 | tf_op jit(solution)/shard_map/ppermute | solution.py:160
  132.8 6.1 %collective-permute-done.27 = f32[40,1280]{1,0:T(8,128)S(1)} collective-permute-done((f32[40,1280]{1,0:T(8,128)S(1)}, f32[40,1280]{1,0:T(8,128)S(1)}, u32[]{:S(2)}, u32[]{:S(2)}) %collective-permute-start.27) | collective-permute-done | bytes 204832 | tf_op jit(solution)/shard_map/ppermute | solution.py:160
  144.4 2.7 %collective-permute-start.31 = (f32[32,1792]{1,0:T(8,128)S(1)}, f32[32,1792]{1,0:T(8,128)S(1)}, u32[]{:S(2)}, u32[]{:S(2)}) collective-permute-start(f32[32,1792]{1,0:T(8,128)S(1)} %pad_maximum_fusion.18), channel_id=1, source_target_pairs={{0,6},{2,0},{4,2},{6,4},{1,7},{3,1},{5,3},{7,5},{8,14},{10,8},{12,... | collective-permute-start | bytes 688136 | tf_op jit(solution)/shard_map/ppermute | solution.py:160
  147.1 5.0 %collective-permute-done.29 = f32[32,1792]{1,0:T(8,128)S(1)} collective-permute-done((f32[32,1792]{1,0:T(8,128)S(1)}, f32[32,1792]{1,0:T(8,128)S(1)}, u32[]{:S(2)}, u32[]{:S(2)}) %collective-permute-start.29) | collective-permute-done | bytes 229408 | tf_op jit(solution)/shard_map/ppermute | solution.py:160
  152.2 5.8 %collective-permute-done.30 = f32[32,1792]{1,0:T(8,128)S(1)} collective-permute-done((f32[32,1792]{1,0:T(8,128)S(1)}, f32[32,1792]{1,0:T(8,128)S(1)}, u32[]{:S(2)}, u32[]{:S(2)}) %collective-permute-start.30) | collective-permute-done | bytes 229408 | tf_op jit(solution)/shard_map/ppermute | solution.py:160
  166.8 1.1 pad_maximum_fusion.4.refs_6_
  168.0 0.9 copy-done.4
  169.1 14.6 %finish.1 = (bf16[2,1152,1152]{2,1,0:T(8,128)(2,1)}, f32[2,144,1152]{2,1,0:T(8,128)}, f32[2,144,1152]{2,1,0:T(8,128)}) custom-call(s32[24]{0:T(128)} %pad_add_fusion.place_ref, bf16[4,152,1152]{2,1,0:T(8,128)(2,1)} %copy-done, bf16[4,152,1152]{2,1,0:T(8,128)(2,1)} %copy-done.1, bf16[4,152,1152]{2,1,0:T(8,128)(2,1)} %copy-done.2, ...), custom_call_target="tpu_custom_call" | custom-call | tf_op jit(solution)/shard_map/finish/pallas_call | solution.py:116
  (186 shorter events, 23.6 us)
Async XLA Ops:
  3.9 27.6 %collective-permute-start = (bf16[152,1152]{1,0:T(8,128)(2,1)}, bf16[152,1152]{1,0:T(8,128)(2,1)}, u32[]{:S(2)}, u32[]{:S(2)}) collective-permute-start(bf16[152,1152]{1,0:T(8,128)(2,1)} %get-tuple-element.72), channel_id=1, source_target_pairs={{0,2},{2,4},{4,6},{6,0},{1,3},{3,5},{5,7},{7,1},{8,10},{10,12},{12... | collective-permute-start | bytes 1050632 | tf_op jit(solution)/shard_map/ppermute | solution.py:160
  6.0 25.5 %collective-permute-start.1 = (bf16[152,1152]{1,0:T(8,128)(2,1)}, bf16[152,1152]{1,0:T(8,128)(2,1)}, u32[]{:S(2)}, u32[]{:S(2)}) collective-permute-start(bf16[152,1152]{1,0:T(8,128)(2,1)} %get-tuple-element.72), channel_id=1, source_target_pairs={{0,4},{2,6},{4,0},{6,2},{1,5},{3,7},{5,1},{7,3},{8,12},{10,14},{12... | collective-permute-start | bytes 1050632 | tf_op jit(solution)/shard_map/ppermute | solution.py:160
  8.6 22.9 %collective-permute-start.2 = (bf16[152,1152]{1,0:T(8,128)(2,1)}, bf16[152,1152]{1,0:T(8,128)(2,1)}, u32[]{:S(2)}, u32[]{:S(2)}) collective-permute-start(bf16[152,1152]{1,0:T(8,128)(2,1)} %get-tuple-element.72), channel_id=1, source_target_pairs={{0,6},{2,0},{4,2},{6,4},{1,7},{3,1},{5,3},{7,5},{8,14},{10,8},{12,... | collective-permute-start | bytes 1050632 | tf_op jit(solution)/shard_map/ppermute | solution.py:160
  24.1 9.2 %collective-permute-start.8 = (bf16[4,144,1152]{2,1,0:T(8,128)(2,1)S(1)}, bf16[4,144,1152]{2,1,0:T(8,128)(2,1)S(1)}, u32[]{:S(2)}, u32[]{:S(2)}) collective-permute-start(bf16[4,144,1152]{2,1,0:T(8,128)(2,1)S(1)} %fusion.10), channel_id=1, source_target_pairs={{0,1},{1,0},{2,3},{3,2},{4,5},{5,4},{6,7},{7,6},{8,9},{9,8},{10,11... | collective-permute-start | bytes 3981320 | tf_op jit(solution)/shard_map/ppermute | solution.py:157
  32.9 14.0 %copy-start = (bf16[4,152,1152]{2,1,0:T(8,128)(2,1)}, bf16[4,152,1152]{2,1,0:T(8,128)(2,1)S(1)}, u32[]{:S(2)}) copy-start(bf16[4,152,1152]{2,1,0:T(8,128)(2,1)S(1)} %pad_maximum_fusion.1.refs_0_) | copy-start | bytes 4202500
  33.0 16.2 %collective-permute-start.6 = (bf16[4,152,1152]{2,1,0:T(8,128)(2,1)S(1)}, bf16[4,152,1152]{2,1,0:T(8,128)(2,1)S(1)}, u32[]{:S(2)}, u32[]{:S(2)}) collective-permute-start(bf16[4,152,1152]{2,1,0:T(8,128)(2,1)S(1)} %pad_maximum_fusion.1.refs_0_), channel_id=1, source_target_pairs={{0,1},{1,0},{2,3},{3,2},{4,5},{5,4},{6,7},{7,6},{8,9},{9,8},{10,11... | collective-permute-start | bytes 4202504 | tf_op jit(solution)/shard_map/ppermute | solution.py:157
  45.3 1.0 copy-start.7
  45.4 3.8 %collective-permute-start.12 = (bf16[4,144,1152]{2,1,0:T(8,128)(2,1)S(1)}, bf16[4,144,1152]{2,1,0:T(8,128)(2,1)S(1)}, u32[]{:S(2)}, u32[]{:S(2)}) collective-permute-start(bf16[4,144,1152]{2,1,0:T(8,128)(2,1)S(1)} %fusion.11), channel_id=1, source_target_pairs={{0,1},{1,0},{2,3},{3,2},{4,5},{5,4},{6,7},{7,6},{8,9},{9,8},{10,11... | collective-permute-start | bytes 3981320 | tf_op jit(solution)/shard_map/ppermute | solution.py:157
  46.9 9.1 %collective-permute-start.10 = (bf16[144,1152]{1,0:T(8,128)(2,1)S(1)}, bf16[144,1152]{1,0:T(8,128)(2,1)S(1)}, u32[]{:S(2)}, u32[]{:S(2)}) collective-permute-start(bf16[144,1152]{1,0:T(8,128)(2,1)S(1)} %get-tuple-element.51), channel_id=1, source_target_pairs={{0,6},{2,0},{4,2},{6,4},{1,7},{3,1},{5,3},{7,5},{8,14},{10,8},{12,... | collective-permute-start | bytes 995336 | tf_op jit(solution)/shard_map/ppermute | solution.py:160
  47.0 10.7 %collective-permute-start.11 = (bf16[144,1152]{1,0:T(8,128)(2,1)S(1)}, bf16[144,1152]{1,0:T(8,128)(2,1)S(1)}, u32[]{:S(2)}, u32[]{:S(2)}) collective-permute-start(bf16[144,1152]{1,0:T(8,128)(2,1)S(1)} %get-tuple-element.52), channel_id=1, source_target_pairs={{0,4},{2,6},{4,0},{6,2},{1,5},{3,7},{5,1},{7,3},{8,12},{10,14},{12... | collective-permute-start | bytes 995336 | tf_op jit(solution)/shard_map/ppermute | solution.py:160
  49.2 16.2 %collective-permute-start.9 = (bf16[144,1152]{1,0:T(8,128)(2,1)S(1)}, bf16[144,1152]{1,0:T(8,128)(2,1)S(1)}, u32[]{:S(2)}, u32[]{:S(2)}) collective-permute-start(bf16[144,1152]{1,0:T(8,128)(2,1)S(1)} %get-tuple-element.53), channel_id=1, source_target_pairs={{0,2},{2,4},{4,6},{6,0},{1,3},{3,5},{5,7},{7,1},{8,10},{10,12},{12... | collective-permute-start | bytes 995336 | tf_op jit(solution)/shard_map/ppermute | solution.py:160
  49.2 1.1 copy-start.2
  49.2 29.8 %copy-start.3 = (f32[1,2,144,1152]{3,2,1,0:T(8,128)S(1)}, f32[1,2,144,1152]{3,2,1,0:T(8,128)}, u32[]{:S(2)}) copy-start(f32[1,2,144,1152]{3,2,1,0:T(8,128)} %param.12) | copy-start | bytes 3981316
  50.3 22.8 %collective-permute-start.13 = (bf16[144,1152]{1,0:T(8,128)(2,1)S(1)}, bf16[144,1152]{1,0:T(8,128)(2,1)S(1)}, u32[]{:S(2)}, u32[]{:S(2)}) collective-permute-start(bf16[144,1152]{1,0:T(8,128)(2,1)S(1)} %get-tuple-element.48), channel_id=1, source_target_pairs={{0,2},{2,4},{4,6},{6,0},{1,3},{3,5},{5,7},{7,1},{8,10},{10,12},{12... | collective-permute-start | bytes 995336 | tf_op jit(solution)/shard_map/ppermute | solution.py:160
  50.8 22.3 %collective-permute-start.14 = (bf16[144,1152]{1,0:T(8,128)(2,1)S(1)}, bf16[144,1152]{1,0:T(8,128)(2,1)S(1)}, u32[]{:S(2)}, u32[]{:S(2)}) collective-permute-start(bf16[144,1152]{1,0:T(8,128)(2,1)S(1)} %get-tuple-element.50), channel_id=1, source_target_pairs={{0,6},{2,0},{4,2},{6,4},{1,7},{3,1},{5,3},{7,5},{8,14},{10,8},{12,... | collective-permute-start | bytes 995336 | tf_op jit(solution)/shard_map/ppermute | solution.py:160
  56.1 23.0 %collective-permute-start.15 = (bf16[144,1152]{1,0:T(8,128)(2,1)S(1)}, bf16[144,1152]{1,0:T(8,128)(2,1)S(1)}, u32[]{:S(2)}, u32[]{:S(2)}) collective-permute-start(bf16[144,1152]{1,0:T(8,128)(2,1)S(1)} %get-tuple-element.49), channel_id=1, source_target_pairs={{0,4},{2,6},{4,0},{6,2},{1,5},{3,7},{5,1},{7,3},{8,12},{10,14},{12... | collective-permute-start | bytes 995336 | tf_op jit(solution)/shard_map/ppermute | solution.py:160
  81.0 3.6 %collective-permute-start.16 = (bf16[152,1152]{1,0:T(8,128)(2,1)S(1)}, bf16[152,1152]{1,0:T(8,128)(2,1)}, u32[]{:S(2)}, u32[]{:S(2)}) collective-permute-start(bf16[152,1152]{1,0:T(8,128)(2,1)S(1)} %get-tuple-element.83), channel_id=1, source_target_pairs={{0,1},{1,0},{2,3},{3,2},{4,5},{5,4},{6,7},{7,6},{8,9},{9,8},{10,11... | collective-permute-start | bytes 1050632 | tf_op jit(solution)/shard_map/ppermute | solution.py:157
  82.4 20.9 %collective-permute-start.4 = (bf16[152,1152]{1,0:T(8,128)(2,1)S(1)}, bf16[152,1152]{1,0:T(8,128)(2,1)S(1)}, u32[]{:S(2)}, u32[]{:S(2)}) collective-permute-start(bf16[152,1152]{1,0:T(8,128)(2,1)S(1)} %get-tuple-element.70), channel_id=1, source_target_pairs={{0,4},{2,6},{4,0},{6,2},{1,5},{3,7},{5,1},{7,3},{8,12},{10,14},{12... | collective-permute-start | bytes 1050632 | tf_op jit(solution)/shard_map/ppermute | solution.py:160
  84.5 20.6 %collective-permute-start.5 = (bf16[152,1152]{1,0:T(8,128)(2,1)S(1)}, bf16[152,1152]{1,0:T(8,128)(2,1)S(1)}, u32[]{:S(2)}, u32[]{:S(2)}) collective-permute-start(bf16[152,1152]{1,0:T(8,128)(2,1)S(1)} %get-tuple-element.70), channel_id=1, source_target_pairs={{0,6},{2,0},{4,2},{6,4},{1,7},{3,1},{5,3},{7,5},{8,14},{10,8},{12,... | collective-permute-start | bytes 1050632 | tf_op jit(solution)/shard_map/ppermute | solution.py:160
  86.6 7.5 %collective-permute-start.17 = (bf16[80,1152]{1,0:T(8,128)(2,1)S(1)}, bf16[80,1152]{1,0:T(8,128)(2,1)S(1)}, u32[]{:S(2)}, u32[]{:S(2)}) collective-permute-start(bf16[80,1152]{1,0:T(8,128)(2,1)S(1)} %get-tuple-element.80), channel_id=1, source_target_pairs={{0,64},{32,96},{64,0},{96,32},{1,65},{33,97},{65,1},{97,33},{2,66}... | collective-permute-start | bytes 552968 | tf_op jit(solution)/shard_map/ppermute | solution.py:160
  89.4 9.2 %collective-permute-start.18 = (bf16[80,1152]{1,0:T(8,128)(2,1)S(1)}, bf16[80,1152]{1,0:T(8,128)(2,1)S(1)}, u32[]{:S(2)}, u32[]{:S(2)}) collective-permute-start(bf16[80,1152]{1,0:T(8,128)(2,1)S(1)} %get-tuple-element.81), channel_id=1, source_target_pairs={{0,32},{32,64},{64,96},{96,0},{1,33},{33,65},{65,97},{97,1},{2,34}... | collective-permute-start | bytes 552968 | tf_op jit(solution)/shard_map/ppermute | solution.py:160
  89.7 8.9 %collective-permute-start.19 = (bf16[80,1152]{1,0:T(8,128)(2,1)S(1)}, bf16[80,1152]{1,0:T(8,128)(2,1)S(1)}, u32[]{:S(2)}, u32[]{:S(2)}) collective-permute-start(bf16[80,1152]{1,0:T(8,128)(2,1)S(1)} %get-tuple-element.82), channel_id=1, source_target_pairs={{0,96},{32,0},{64,32},{96,64},{1,97},{33,1},{65,33},{97,65},{2,98}... | collective-permute-start | bytes 552968 | tf_op jit(solution)/shard_map/ppermute | solution.py:160
  94.1 11.1 %collective-permute-start.3 = (bf16[152,1152]{1,0:T(8,128)(2,1)S(1)}, bf16[152,1152]{1,0:T(8,128)(2,1)S(1)}, u32[]{:S(2)}, u32[]{:S(2)}) collective-permute-start(bf16[152,1152]{1,0:T(8,128)(2,1)S(1)} %get-tuple-element.70), channel_id=1, source_target_pairs={{0,2},{2,4},{4,6},{6,0},{1,3},{3,5},{5,7},{7,1},{8,10},{10,12},{12... | collective-permute-start | bytes 1050632 | tf_op jit(solution)/shard_map/ppermute | solution.py:160
  98.8 8.1 %collective-permute-start.20 = (bf16[80,1152]{1,0:T(8,128)(2,1)S(1)}, bf16[80,1152]{1,0:T(8,128)(2,1)S(1)}, u32[]{:S(2)}, u32[]{:S(2)}) collective-permute-start(bf16[80,1152]{1,0:T(8,128)(2,1)S(1)} %pad_maximum_fusion.8), channel_id=1, source_target_pairs={{0,16},{8,24},{16,0},{24,8},{1,17},{9,25},{17,1},{25,9},{2,18},{10... | collective-permute-start | bytes 552968 | tf_op jit(solution)/shard_map/ppermute | solution.py:160
  102.5 8.7 %collective-permute-start.21 = (bf16[80,1152]{1,0:T(8,128)(2,1)S(1)}, bf16[80,1152]{1,0:T(8,128)(2,1)S(1)}, u32[]{:S(2)}, u32[]{:S(2)}) collective-permute-start(bf16[80,1152]{1,0:T(8,128)(2,1)S(1)} %pad_maximum_fusion.8), channel_id=1, source_target_pairs={{0,8},{8,16},{16,24},{24,0},{1,9},{9,17},{17,25},{25,1},{2,10},{10... | collective-permute-start | bytes 552968 | tf_op jit(solution)/shard_map/ppermute | solution.py:160
  103.2 8.0 %collective-permute-start.22 = (bf16[80,1152]{1,0:T(8,128)(2,1)S(1)}, bf16[80,1152]{1,0:T(8,128)(2,1)S(1)}, u32[]{:S(2)}, u32[]{:S(2)}) collective-permute-start(bf16[80,1152]{1,0:T(8,128)(2,1)S(1)} %pad_maximum_fusion.8), channel_id=1, source_target_pairs={{0,24},{8,0},{16,8},{24,16},{1,25},{9,1},{17,9},{25,17},{2,26},{10... | collective-permute-start | bytes 552968 | tf_op jit(solution)/shard_map/ppermute | solution.py:160
  105.4 24.0 %copy-start.1 = (bf16[4,152,1152]{2,1,0:T(8,128)(2,1)}, bf16[4,152,1152]{2,1,0:T(8,128)(2,1)S(1)}, u32[]{:S(2)}) copy-start(bf16[4,152,1152]{2,1,0:T(8,128)(2,1)S(1)} %pad_maximum_fusion.2.refs_1_) | copy-start | bytes 4202500
  105.4 57.5 %collective-permute-start.7 = (bf16[4,152,1152]{2,1,0:T(8,128)(2,1)S(1)}, bf16[4,152,1152]{2,1,0:T(8,128)(2,1)}, u32[]{:S(2)}, u32[]{:S(2)}) collective-permute-start(bf16[4,152,1152]{2,1,0:T(8,128)(2,1)S(1)} %pad_maximum_fusion.2.refs_1_), channel_id=1, source_target_pairs={{0,1},{1,0},{2,3},{3,2},{4,5},{5,4},{6,7},{7,6},{8,9},{9,8},{10,11... | collective-permute-start | bytes 4202504 | tf_op jit(solution)/shard_map/ppermute | solution.py:157
  111.4 5.8 %collective-permute-start.23 = (bf16[72,1152]{1,0:T(8,128)(2,1)S(1)}, bf16[72,1152]{1,0:T(8,128)(2,1)S(1)}, u32[]{:S(2)}, u32[]{:S(2)}) collective-permute-start(bf16[72,1152]{1,0:T(8,128)(2,1)S(1)} %add_convert_fusion.6), channel_id=1, source_target_pairs={{0,96},{32,0},{64,32},{96,64},{1,97},{33,1},{65,33},{97,65},{2,98}... | collective-permute-start | bytes 497672 | tf_op jit(solution)/shard_map/ppermute | solution.py:160
  113.5 5.8 %collective-permute-start.24 = (bf16[72,1152]{1,0:T(8,128)(2,1)S(1)}, bf16[72,1152]{1,0:T(8,128)(2,1)S(1)}, u32[]{:S(2)}, u32[]{:S(2)}) collective-permute-start(bf16[72,1152]{1,0:T(8,128)(2,1)S(1)} %add_convert_fusion.6), channel_id=1, source_target_pairs={{0,64},{32,96},{64,0},{96,32},{1,65},{33,97},{65,1},{97,33},{2,66}... | collective-permute-start | bytes 497672 | tf_op jit(solution)/shard_map/ppermute | solution.py:160
  114.5 9.3 %collective-permute-start.25 = (bf16[72,1152]{1,0:T(8,128)(2,1)S(1)}, bf16[72,1152]{1,0:T(8,128)(2,1)S(1)}, u32[]{:S(2)}, u32[]{:S(2)}) collective-permute-start(bf16[72,1152]{1,0:T(8,128)(2,1)S(1)} %add_convert_fusion.6), channel_id=1, source_target_pairs={{0,32},{32,64},{64,96},{96,0},{1,33},{33,65},{65,97},{97,1},{2,34}... | collective-permute-start | bytes 497672 | tf_op jit(solution)/shard_map/ppermute | solution.py:160
  123.9 0.9 copy-start.6
  125.9 6.9 %collective-permute-start.26 = (f32[40,1280]{1,0:T(8,128)S(1)}, f32[40,1280]{1,0:T(8,128)S(1)}, u32[]{:S(2)}, u32[]{:S(2)}) collective-permute-start(f32[40,1280]{1,0:T(8,128)S(1)} %select_maximum_fusion.1), channel_id=1, source_target_pairs={{0,4},{2,6},{4,0},{6,2},{1,5},{3,7},{5,1},{7,3},{8,12},{10,14},{12... | collective-permute-start | bytes 614408 | tf_op jit(solution)/shard_map/ppermute | solution.py:160
  126.7 12.2 %collective-permute-start.27 = (f32[40,1280]{1,0:T(8,128)S(1)}, f32[40,1280]{1,0:T(8,128)S(1)}, u32[]{:S(2)}, u32[]{:S(2)}) collective-permute-start(f32[40,1280]{1,0:T(8,128)S(1)} %select_maximum_fusion.1), channel_id=1, source_target_pairs={{0,2},{2,4},{4,6},{6,0},{1,3},{3,5},{5,7},{7,1},{8,10},{10,12},{12... | collective-permute-start | bytes 614408 | tf_op jit(solution)/shard_map/ppermute | solution.py:160
  126.8 12.1 %collective-permute-start.28 = (f32[40,1280]{1,0:T(8,128)S(1)}, f32[40,1280]{1,0:T(8,128)S(1)}, u32[]{:S(2)}, u32[]{:S(2)}) collective-permute-start(f32[40,1280]{1,0:T(8,128)S(1)} %select_maximum_fusion.1), channel_id=1, source_target_pairs={{0,6},{2,0},{4,2},{6,4},{1,7},{3,1},{5,3},{7,5},{8,14},{10,8},{12,... | collective-permute-start | bytes 614408 | tf_op jit(solution)/shard_map/ppermute | solution.py:160
  143.9 8.3 %collective-permute-start.29 = (f32[32,1792]{1,0:T(8,128)S(1)}, f32[32,1792]{1,0:T(8,128)S(1)}, u32[]{:S(2)}, u32[]{:S(2)}) collective-permute-start(f32[32,1792]{1,0:T(8,128)S(1)} %pad_maximum_fusion.18), channel_id=1, source_target_pairs={{0,4},{2,6},{4,0},{6,2},{1,5},{3,7},{5,1},{7,3},{8,12},{10,14},{12... | collective-permute-start | bytes 688136 | tf_op jit(solution)/shard_map/ppermute | solution.py:160
  144.4 13.5 %collective-permute-start.30 = (f32[32,1792]{1,0:T(8,128)S(1)}, f32[32,1792]{1,0:T(8,128)S(1)}, u32[]{:S(2)}, u32[]{:S(2)}) collective-permute-start(f32[32,1792]{1,0:T(8,128)S(1)} %pad_maximum_fusion.18), channel_id=1, source_target_pairs={{0,2},{2,4},{4,6},{6,0},{1,3},{3,5},{5,7},{7,1},{8,10},{10,12},{12... | collective-permute-start | bytes 688136 | tf_op jit(solution)/shard_map/ppermute | solution.py:160
  144.4 13.5 %collective-permute-start.31 = (f32[32,1792]{1,0:T(8,128)S(1)}, f32[32,1792]{1,0:T(8,128)S(1)}, u32[]{:S(2)}, u32[]{:S(2)}) collective-permute-start(f32[32,1792]{1,0:T(8,128)S(1)} %pad_maximum_fusion.18), channel_id=1, source_target_pairs={{0,6},{2,0},{4,2},{6,4},{1,7},{3,1},{5,3},{7,5},{8,14},{10,8},{12,... | collective-permute-start | bytes 688136 | tf_op jit(solution)/shard_map/ppermute | solution.py:160
  162.3 2.1 %collective-permute-start.32 = (f32[40,3200]{1,0:T(8,128)S(1)}, f32[40,3200]{1,0:T(8,128)S(1)}, u32[]{:S(2)}, u32[]{:S(2)}) collective-permute-start(f32[40,3200]{1,0:T(8,128)S(1)} %select_maximum_fusion), channel_id=1, source_target_pairs={{0,1},{1,0},{2,3},{3,2},{4,5},{5,4},{6,7},{7,6},{8,9},{9,8},{10,11... | collective-permute-start | bytes 1536008 | tf_op jit(solution)/shard_map/ppermute | solution.py:157
  164.8 0.7 copy-start.8
  168.0 0.9 copy-start.4
  168.0 1.2 copy-start.5
where the time goes:
time: 185 us; the launch traced here: 184 us
  waiting for transfers between devices  64.2 us (35%)
  starting transfers between devices  41.9 us (23%)
  matrix products  29.8 us (16%)
  other arithmetic  23.1 us (12%)
  Pallas kernels  14.6 us (8%)
  local copies, waits for them, and re-layouts  6.97 us (4%)
  between operations  3.31 us (2%)
    ppermute x27, waiting for transfers between devices, from_back(): return lax.ppermute(value, axis, ring(4, step))  63.6 us
    ppermute x27, starting transfers between devices, from_back(): return lax.ppermute(value, axis, ring(4, step))  36.3 us
    dot_general x2, matrix products, chip_blocks(): jnp.einsum('tr,te->re', x[layer], y[layer], preferred_element_type=F32)  22.6 us
    pallas_call x1, Pallas kernels, finish(): pl.pallas_call(functools.partial(final_kernel, reps, ys), out_shape=(jax....  14.6 us
    ppermute x6, starting transfers between devices, swap(): return lax.ppermute(value, 'core', ring(cores, 1))  5.6 us
    reduce_sum x1, other arithmetic, body(): col_sums = jnp.sum(out_grads, axis=1, dtype=F32)  4.97 us
  transfers between devices with their start and end apart: 33, of which 17 were waited for; matrix products, arithmetic and copies ran while one was open for 26% of the time, Pallas kernels for 0%

commit v1 on v0

v1 whole, which is shorter than its diff:
```python
import jax
import jax.numpy as jnp
from jax import lax
from jax.sharding import Mesh
from jax.sharding import PartitionSpec as P


ROUNDS = 2
NS_STEPS = 5
HIGH = lax.Precision.HIGHEST
BF = jnp.bfloat16
F32 = jnp.float32


def ring(count, step):
    return [(i, (i + step) % count) for i in range(count)]


def pick(stack, index, axis=0):
    return lax.dynamic_index_in_dim(stack, index, axis, keepdims=False)


def hi_lo(row):
    high = row.astype(BF)
    low = (row - high.astype(F32)).astype(BF)
    return jnp.concatenate([high[None], low[None], jnp.zeros((6, row.shape[0]), BF)], 0)


def from_hi_lo(rows):
    return rows[0].astype(F32) + rows[1].astype(F32)


def paired(parts):
    return (parts[0] + parts[1]) + (parts[2] + parts[3])


def split3(value):
    one = value.astype(BF)
    rest = value - one.astype(F32)
    two = rest.astype(BF)
    three = (rest - two.astype(F32)).astype(BF)
    return jnp.concatenate([one, two, three], 0)


def by_three(left, right, dims):
    rank = left.shape[0]
    out = lax.dot_general(split3(left), right, dims, preferred_element_type=F32)
    return out[:rank] + out[rank : 2 * rank] + out[2 * rank :]


def inverse_root(gram):
    fro = jnp.sqrt(jnp.sum(gram * gram)) + 1e-06
    eye = jnp.eye(gram.shape[-1], dtype=F32)
    ymat = gram / fro
    zmat = eye
    for _ in range(NS_STEPS):
        tmat = 1.5 * eye - 0.5 * jnp.dot(zmat, ymat, precision=HIGH)
        ymat = jnp.dot(ymat, tmat, precision=HIGH)
        zmat = jnp.dot(tmat, zmat, precision=HIGH)
    return zmat, jnp.sqrt(fro)


def products(left, right):
    l1 = left.astype(BF)
    rest = left - l1.astype(F32)
    l2 = rest.astype(BF)
    l3 = (rest - l2.astype(F32)).astype(BF)
    r1 = right.astype(BF)
    rest = right - r1.astype(F32)
    r2 = rest.astype(BF)
    r3 = (rest - r2.astype(F32)).astype(BF)
    return (
        jnp.concatenate([l1, l1, l2, l1, l2, l3], -2),
        jnp.concatenate([r1, r2, r1, r3, r2, r1], -2),
    )


def body(inputs, out_grads, weights, biases, errors, momenta, bias_momenta, q_start):
    layers, tok, width = inputs.shape
    cores = lax.axis_size("core")
    ys = lax.axis_size("y")
    xs = lax.axis_size("x")
    reps = xs * lax.axis_size("z")
    rows = width // (cores * ys)
    rank = q_start.shape[-1]
    scale = float(tok) ** (-0.5)
    core, ypos, xpos = lax.axis_index("core"), lax.axis_index("y"), lax.axis_index("x")

    def swap(value):
        return lax.ppermute(value, "core", ring(cores, 1))

    def trade(value, axis, k):
        return lax.ppermute(value, axis, [(i, i ^ k) for i in range(4)])

    def everyone(value, axis):
        return [value] + [trade(value, axis, k) for k in (1, 2, 3)]

    def natural(parts, position):
        ordered = []
        for j in range(4):
            value = parts[j]
            for spot in (1, 2, 3):
                value = jnp.where(position == spot, parts[spot ^ j], value)
            ordered.append(value)
        return ordered

    old_m = lax.optimization_barrier(momenta)
    old = (weights.astype(F32) - 0.45 * old_m).astype(BF)
    row_b, row_m = lax.optimization_barrier((biases, bias_momenta))
    two = jnp.stack([row_b, row_m.astype(BF)], 1)
    old = jnp.concatenate([old, jnp.pad(two, ((0, 0), (0, 6), (0, width - rows)))], 1)
    parts = everyone(old, "y")
    mine = jnp.stack(natural(parts, ypos))
    theirs = swap(mine)
    even, odd = jnp.where(core == 0, mine, theirs), jnp.where(core == 0, theirs, mine)
    old = jnp.stack([even, odd], 1)
    old_b = old[:, :, :, rows, :rows].astype(F32) - 0.45 * old[:, :, :, rows + 1, :rows].astype(F32)
    old_b = old_b.transpose(2, 0, 1, 3).reshape(layers, width)
    old = old[:, :, :, :rows].transpose(2, 0, 1, 3, 4).reshape(layers, width, width)
    old, old_b = lax.optimization_barrier((old, old_b))

    def chip_blocks(layer, after=None):
        x, y = inputs, out_grads
        if after is not None:
            x, y, _ = lax.optimization_barrier((x, y, after))
        part = jnp.einsum("tr,te->re", x[layer], y[layer], preferred_element_type=F32).astype(BF)
        part = lax.optimization_barrier(part).reshape(ys * cores, rows, width)
        got = swap(
            pick(part.reshape(ys, cores, rows, width), 1 - core, 1)
        )
        blocks = []
        for k in range(4):
            there = ypos ^ k
            blocks.append(pick(part, there * cores + core).astype(F32) + pick(got, there).astype(F32))
        return blocks[0], [b.astype(BF) for b in blocks[1:]]

    def merge(layer, own, blocks):
        for k in (1, 2, 3):
            block = trade(blocks[k - 1], "y", k)
            own = own + block.astype(F32)
        return own * scale + errors[0, layer]

    own0, blocks0 = chip_blocks(0)
    own1, blocks1 = chip_blocks(1, blocks0)
    merged = jnp.stack([merge(0, own0, blocks0), merge(1, own1, blocks1)])
    col_sums = jnp.sum(out_grads, axis=1, dtype=F32)

    got = swap(
        jnp.concatenate([pick(merged, 1 - core).astype(BF), hi_lo(pick(col_sums, 1 - core))], 0)
    )
    both = jnp.stack([pick(merged, core), got[:rows].astype(F32)]).reshape(4, rows // 2, width)
    bias = pick(col_sums, core) + from_hi_lo(got[rows:])
    bias_rows = hi_lo(bias)
    half = rows // 2

    def loaded(main):
        return jnp.concatenate([main.astype(BF), bias_rows], 0)

    parts = []
    for k in (1, 2, 3):
        block = loaded(pick(both, xpos ^ k))
        parts.append(trade(block, "x", k))
    main = paired([pick(both, xpos)] + [p[:half].astype(F32) for p in parts])
    bias = paired([from_hi_lo(p) for p in [bias_rows] + [p[half:] for p in parts]])
    bias_rows = hi_lo(bias)
    parts = everyone(loaded(main), "z")
    main = paired([p[:half].astype(F32) for p in parts]).astype(BF)
    bias = paired([from_hi_lo(p[half:]) for p in parts])
    parts = everyone(main, "x")
    quarter = natural(parts, xpos)
    total = jnp.concatenate(quarter, 0)

    q = pick(q_start, core).T
    for rnd in range(ROUNDS):
        p = by_three(q, total, (((1,), (1,)), ((), ())))
        gram = lax.dot_general(p, p, (((1,), (1,)), ((), ())), precision=HIGH)
        u = by_three(p, total, (((1,), (0,)), ((), ())))
        gram = jnp.pad(gram, ((0, 0), (0, 128 - rank)))
        if rnd == 0:
            wide = gram
        else:
            wide = jnp.concatenate([gram, jnp.pad(p, ((0, 0), (0, 384 - 2 * rows)))], 1)
        high = wide.astype(BF)
        packed = jnp.concatenate([u.astype(BF), high, (wide - high.astype(F32)).astype(BF)], 1)
        if rnd == 0:
            last = jnp.pad(hi_lo(bias), ((0, 0), (0, 256)))
            packed = jnp.concatenate([packed, last], 0)
        parts = everyone(packed, "y")
        span = wide.shape[1]
        wides = [
            part[:rank, width : width + span].astype(F32) + part[:rank, width + span :].astype(F32)
            for part in parts
        ]
        u = paired([part[:rank, :width].astype(F32) for part in parts])
        gram = paired([wide[:, :rank] for wide in wides])
        zmat, root = inverse_root(gram)
        q = lax.dot_general(zmat, u, (((0,), (0,)), ((), ())), precision=HIGH) / root
        if rnd == 0:
            bias = paired([from_hi_lo(part[rank:, :width]) for part in parts])
    p_all = natural([wide[:, 128 : 128 + 2 * rows] for wide in wides], ypos)
    p_all = jnp.concatenate(p_all, 1)
    phat = lax.dot_general(zmat, p_all, (((0,), (0,)), ((), ())), precision=HIGH) / root

    last = jnp.concatenate([bias[None], jnp.zeros((1, phat.shape[1]), F32)], 1)
    packed = jnp.concatenate(
        [jnp.concatenate([q, phat], 1), jnp.pad(last, ((0, 7), (0, 0)))], 0
    )
    other = swap(packed)
    pair = [jnp.where(core == layer, packed, other) for layer in range(layers)]
    bias = jnp.stack([p[rank, :width] for p in pair])
    q = jnp.stack([p[:rank, :width] for p in pair])
    phat = [p[:rank, width:].reshape(rank, ys, cores, rows) for p in pair]
    phat = jnp.stack([phat[0], phat[1][:, :, ::-1]]).reshape(layers, rank, width)
    left, right = products(phat, q)
    grp = ypos * cores + core
    own = lax.dynamic_slice_in_dim(left, grp * rows, rows, 2)
    spec = "lkr,lke->lre"
    approx = jnp.einsum(spec, own, right, preferred_element_type=F32) * (1.0 / reps)
    new_errors = merged - approx
    new_momenta = 0.9 * momenta + approx
    whole = jnp.einsum(spec, left, right, preferred_element_type=F32) * (1.0 / reps)
    new_weights = (old.astype(F32) - 0.5 * whole).astype(BF)

    bias_grad = bias * (scale / reps)
    new_bias_momenta = 0.9 * bias_momenta + lax.dynamic_slice_in_dim(bias_grad, grp * rows, rows, 1)
    new_biases = (old_b - 0.5 * bias_grad).astype(BF)
    return (new_weights, new_biases, new_errors[None], new_momenta, new_bias_momenta)


def solution(mesh):
    split = Mesh(mesh.devices.reshape(4, 4, 4, 2), ("x", "z", "y", "core"))
    rep, grp = ("x", "z"), ("y", "core")
    placed = (
        P(None, rep + grp, None),
        P(None, rep + grp, None),
        P(None, grp, None),
        P(None, grp),
        P(rep, None, grp, None),
        P(None, grp, None),
        P(None, grp),
        P(),
    )

    return jax.shard_map(
        body,
        mesh=split,
        in_specs=placed,
        out_specs=(P(), P(), P(rep, None, grp, None), P(None, grp, None), P(None, grp)),
        check_vma=False,
    )
```

time: 185 us -> 186 us (level)
  Pallas kernels: 14.6 us -> 0 us
  matrix products: 29.8 us -> 40.1 us
  waiting for transfers between devices: 64.2 us -> 59.3 us
  local copies, waits for them, and re-layouts: 6.97 us -> 11.5 us
  starting transfers between devices: 41.9 us -> 45.2 us
  other arithmetic: 23.1 us -> 25.9 us
    pallas_call x1 -> x0, Pallas kernels: 14.6 us -> none  [finish(): pl.pallas_call(functools.partial(final_kernel, reps, ys), out_shape=(jax....]
    ppermute x27 -> x24, waiting for transfers between devices: 63.6 us -> 55.2 us  [trade(): return lax.ppermute(value, axis, [(i, i ^ k) for i in range(4)])]
    dot_general x2 -> x4, matrix products: 0.69 us -> 9.11 us  [the longest x1 4.22 us: body(): jnp.einsum(spec, left, right, preferred_element_type=F32) * (1.0 / reps)]
    ppermute x6 -> x5, starting transfers between devices: 5.6 us -> 10.7 us  [swap(): return lax.ppermute(value, 'core', ring(cores, 1))]
    reduce_sum x1, other arithmetic: 4.97 us -> 1.29 us  [body(): col_sums = jnp.sum(out_grads, axis=1, dtype=F32)]
    ppermute x6 -> x5, waiting for transfers between devices: 0.62 us -> 4.09 us  [swap(): return lax.ppermute(value, 'core', ring(cores, 1))]
    transpose x0 -> x2, local copies, waits for them, and re-layouts: none -> 2.79 us  [the longest x1 2.78 us: body(): old[:, :, :, :rows].transpose(2, 0, 1, 3, 4).reshape(layers, width, width)]
    transpose x0 -> x1, other arithmetic: none -> 2.74 us  [body(): old[:, :, :, :rows].transpose(2, 0, 1, 3, 4).reshape(layers, width, width)]
  transfers between devices with their start and end apart: 33 -> 29, of which waited for: 17 -> 15; matrix products, arithmetic and copies ran while one was open for 26% -> 11% of each run, Pallas kernels for 0% -> 0%
where the time goes in v1:
time: 186 us; the launch traced here: 185 us
  waiting for transfers between devices  59.3 us (32%)
  starting transfers between devices  45.2 us (24%)
  matrix products  40.1 us (22%)
  other arithmetic  25.9 us (14%)
  local copies, waits for them, and re-layouts  11.5 us (6%)
  between operations  3.07 us (2%)
    ppermute x24, waiting for transfers between devices, trade(): return lax.ppermute(value, axis, [(i, i ^ k) for i in range(4)])  55.2 us
    ppermute x24, starting transfers between devices, trade(): return lax.ppermute(value, axis, [(i, i ^ k) for i in range(4)])  34.5 us
    dot_general x2, matrix products, chip_blocks(): jnp.einsum('tr,te->re', x[layer], y[layer], preferred_element_type=F32)  20.4 us
    ppermute x5, starting transfers between devices, swap(): return lax.ppermute(value, 'core', ring(cores, 1))  10.7 us
    convert_element_type x2, other arithmetic, chip_blocks(): return (blocks[0], [b.astype(BF) for b in blocks[1:]])  4.64 us
    dot_general x1, matrix products, body(): jnp.einsum(spec, left, right, preferred_element_type=F32) * (1.0 / reps)  4.22 us
    ppermute x5, waiting for transfers between devices, swap(): return lax.ppermute(value, 'core', ring(cores, 1))  4.09 us
  transfers between devices with their start and end apart: 29, of which 15 were waited for; matrix products, arithmetic and copies ran while one was open for 11% of the time, Pallas kernels for 0%

profile of v1, /device:TPU:1, one launch (start us, length us, event | category | flops | bytes accessed | tf_op | source)
XLA Modules:
  0.0 185.0 jit_solution(17533714936248345450)
XLA Ops:
  0.6 10.1 %convolution_convert_fusion.1 = bf16[1152,1152]{1,0:T(8,128)(2,1)S(1)} fusion(bf16[2,2048,1152]{2,1,0:T(8,128)(2,1)} %param.9, bf16[2,2048,1152]{2,1,0:T(8,128)(2,1)} %param.8), kind=kOutput, calls=%fused_computation.5 | convolution fusion | flops 5437145088 | bytes 12091392 | tf_op jit(solution)/shard_map/tr,te->re/dot_general | solution.py:126
  10.8 1.3 dynamic-slice_bitcast_fusion.1
  12.1 1.4 collective-permute-start.4
  13.4 3.0 %collective-permute-done.4 = bf16[4,144,1152]{2,1,0:T(8,128)(2,1)} collective-permute-done((bf16[4,144,1152]{2,1,0:T(8,128)(2,1)}, bf16[4,144,1152]{2,1,0:T(8,128)(2,1)}, u32[]{:S(2)}, u32[]{:S(2)}) %collective-permute-start.4) | collective-permute-done | bytes 1327136 | tf_op jit(solution)/shard_map/ppermute | solution.py:90
  16.5 2.3 %fusion.39 = (bf16[144,1152]{1,0:T(8,128)(2,1)}, bf16[144,1152]{1,0:T(8,128)(2,1)}, bf16[144,1152]{1,0:T(8,128)(2,1)}) fusion(bf16[4,144,1152]{2,1,0:T(8,128)(2,1)} %collective-permute-done.4, s32[]{:T(128)S(6)} %select_n.289, bf16[8,144,1152]{2,1,0:T(8,128)(2,1)S(1)} %bitcast.194, s32[]{:T(128)S(6)} %select_n.288, s32[]{:T(128)S(6)} %select_n.287, ...), kind=kLoop, calls=%fused_computation.97 | loop fusion | flops 1990656 | bytes 2986008 | tf_op jit(solution)/shard_map/convert_element_type | solution.py:135
  18.8 10.3 %convolution_convert_fusion = bf16[1152,1152]{1,0:T(8,128)(2,1)S(1)} fusion(bf16[2,2048,1152]{2,1,0:T(8,128)(2,1)} %param.9, bf16[2,2048,1152]{2,1,0:T(8,128)(2,1)} %param.8), kind=kOutput, calls=%fused_computation.4 | convolution fusion | flops 5437145088 | bytes 12091392 | tf_op jit(solution)/shard_map/tr,te->re/dot_general | solution.py:126
  29.0 1.5 copy-done.6
  32.0 1.3 convert_reduce_fusion
  33.6 3.0 %collective-permute-start.7 = (bf16[144,1152]{1,0:T(8,128)(2,1)}, bf16[144,1152]{1,0:T(8,128)(2,1)S(1)}, u32[]{:S(2)}, u32[]{:S(2)}) collective-permute-start(bf16[144,1152]{1,0:T(8,128)(2,1)} %get-tuple-element.39), channel_id=1, source_target_pairs={{0,6},{2,4},{4,2},{6,0},{1,7},{3,5},{5,3},{7,1},{8,14},{10,12},{12... | collective-permute-start | bytes 995336 | tf_op jit(solution)/shard_map/ppermute | solution.py:93
  37.5 2.3 %fusion.40 = (bf16[144,1152]{1,0:T(8,128)(2,1)}, bf16[144,1152]{1,0:T(8,128)(2,1)}, bf16[144,1152]{1,0:T(8,128)(2,1)}) fusion(bf16[4,144,1152]{2,1,0:T(8,128)(2,1)S(1)} %collective-permute-done.8, s32[]{:T(128)S(6)} %select_n.285, bf16[8,144,1152]{2,1,0:T(8,128)(2,1)} %bitcast.197, s32[]{:T(128)S(6)} %select_n.284, s32[]{:T(128)S(6)} %select_n.289, ...), kind=kLoop, calls=%fused_computation.98 | loop fusion | flops 1990656 | bytes 2986008 | tf_op jit(solution)/shard_map/convert_element_type | solution.py:135
  40.9 1.7 collective-permute-start.11
  42.6 9.2 %collective-permute-done.7 = bf16[144,1152]{1,0:T(8,128)(2,1)S(1)} collective-permute-done((bf16[144,1152]{1,0:T(8,128)(2,1)}, bf16[144,1152]{1,0:T(8,128)(2,1)S(1)}, u32[]{:S(2)}, u32[]{:S(2)}) %collective-permute-start.7) | collective-permute-done | bytes 331808 | tf_op jit(solution)/shard_map/ppermute | solution.py:93
  51.8 1.4 collective-permute-start.10
  54.1 1.7 collective-permute-start.2
  56.4 3.3 %collective-permute-done.9 = bf16[144,1152]{1,0:T(8,128)(2,1)S(1)} collective-permute-done((bf16[144,1152]{1,0:T(8,128)(2,1)}, bf16[144,1152]{1,0:T(8,128)(2,1)S(1)}, u32[]{:S(2)}, u32[]{:S(2)}) %collective-permute-start.9) | collective-permute-done | bytes 331808 | tf_op jit(solution)/shard_map/ppermute | solution.py:93
  59.7 2.1 %collective-permute-start = (bf16[2,152,1152]{2,1,0:T(8,128)(2,1)}, bf16[2,152,1152]{2,1,0:T(8,128)(2,1)}, u32[]{:S(2)}, u32[]{:S(2)}) collective-permute-start(bf16[2,152,1152]{2,1,0:T(8,128)(2,1)} %fusion.25), channel_id=1, source_target_pairs={{0,6},{2,4},{4,2},{6,0},{1,7},{3,5},{5,3},{7,1},{8,14},{10,12},{12... | collective-permute-start | bytes 2101256 | tf_op jit(solution)/shard_map/ppermute | solution.py:93
  61.9 6.8 %collective-permute-done.10 = bf16[144,1152]{1,0:T(8,128)(2,1)} collective-permute-done((bf16[144,1152]{1,0:T(8,128)(2,1)}, bf16[144,1152]{1,0:T(8,128)(2,1)}, u32[]{:S(2)}, u32[]{:S(2)}) %collective-permute-start.10) | collective-permute-done | bytes 331808 | tf_op jit(solution)/shard_map/ppermute | solution.py:93
  68.7 2.6 %fusion.33 = (f32[1,144,1152]{2,1,0:T(8,128)S(1)}, f32[1,144,1152]{2,1,0:T(8,128)S(1)}) fusion(f32[1,2,144,1152]{3,2,1,0:T(8,128)} %param.12, bf16[144,1152]{1,0:T(8,128)(2,1)} %copy-done.10, bf16[144,1152]{1,0:T(8,128)(2,1)} %copy-done.11, bf16[144,1152]{1,0:T(8,128)(2,1)} %copy-done.12, bf16[4,144,1152]{2,1,0:T(8,128)(2,1)} %collective-permute-done.4, ...), kind=kLoop, calls=%fused_computation.77 | loop fusion | flops 3649536 | bytes 5971976 | tf_op jit(solution)/shard_map/stack | solution.py:145
  71.6 2.2 %collective-permute-start.12 = (bf16[152,1152]{1,0:T(8,128)(2,1)S(1)}, bf16[152,1152]{1,0:T(8,128)(2,1)S(1)}, u32[]{:S(2)}, u32[]{:S(2)}) collective-permute-start(bf16[152,1152]{1,0:T(8,128)(2,1)S(1)} %pad_maximum_fusion.8), channel_id=1, source_target_pairs={{0,1},{1,0},{2,3},{3,2},{4,5},{5,4},{6,7},{7,6},{8,9},{9,8},{10,11... | collective-permute-start | bytes 1050632 | tf_op jit(solution)/shard_map/ppermute | solution.py:90
  75.4 1.3 collective-permute-start.13
  76.7 2.4 %collective-permute-start.14 = (bf16[80,1152]{1,0:T(8,128)(2,1)S(1)}, bf16[80,1152]{1,0:T(8,128)(2,1)S(1)}, u32[]{:S(2)}, u32[]{:S(2)}) collective-permute-start(bf16[80,1152]{1,0:T(8,128)(2,1)S(1)} %get-tuple-element.83), channel_id=1, source_target_pairs={{0,64},{32,96},{64,0},{96,32},{1,65},{33,97},{65,1},{97,33},{2,66}... | collective-permute-start | bytes 552968 | tf_op jit(solution)/shard_map/ppermute | solution.py:93
  79.1 2.8 %collective-permute-done.2 = bf16[2,152,1152]{2,1,0:T(8,128)(2,1)} collective-permute-done((bf16[2,152,1152]{2,1,0:T(8,128)(2,1)}, bf16[2,152,1152]{2,1,0:T(8,128)(2,1)}, u32[]{:S(2)}, u32[]{:S(2)}) %collective-permute-start.2) | collective-permute-done | bytes 700448 | tf_op jit(solution)/shard_map/ppermute | solution.py:93
  82.0 2.5 %collective-permute-start.15 = (bf16[80,1152]{1,0:T(8,128)(2,1)S(1)}, bf16[80,1152]{1,0:T(8,128)(2,1)S(1)}, u32[]{:S(2)}, u32[]{:S(2)}) collective-permute-start(bf16[80,1152]{1,0:T(8,128)(2,1)S(1)} %get-tuple-element.84), channel_id=1, source_target_pairs={{0,96},{32,64},{64,32},{96,0},{1,97},{33,65},{65,33},{97,1},{2,98}... | collective-permute-start | bytes 552968 | tf_op jit(solution)/shard_map/ppermute | solution.py:93
  84.4 14.3 %collective-permute-done.1 = bf16[2,152,1152]{2,1,0:T(8,128)(2,1)} collective-permute-done((bf16[2,152,1152]{2,1,0:T(8,128)(2,1)}, bf16[2,152,1152]{2,1,0:T(8,128)(2,1)}, u32[]{:S(2)}, u32[]{:S(2)}) %collective-permute-start.1) | collective-permute-done | bytes 700448 | tf_op jit(solution)/shard_map/ppermute | solution.py:93
  98.7 2.4 %select_bitcast_fusion.5 = (bf16[1,2,152,1152]{3,2,1,0:T(8,128)(2,1)S(1)}, bf16[1,2,152,1152]{3,2,1,0:T(8,128)(2,1)S(1)}, bf16[1,2,152,1152]{3,2,1,0:T(8,128)(2,1)S(1)}, bf16[1,2,152,1152]{3,2,1,0:T(8,128)(2,1)S(1)}) fusion(bf16[2,152,1152]{2,1,0:T(8,128)(2,1)} %collective-permute-done, bf16[2,152,1152]{2,1,0:T(8,128)(2,1)} %collective-permute-done.1, ...), kind=kLoop, calls=%fused_computation.65 | loop fusion | flops 6303744 | bytes 5567619 | tf_op jit(solution)/shard_map/stack | solution.py:113
  101.3 3.8 %collective-permute-start.18 = (bf16[80,1152]{1,0:T(8,128)(2,1)S(1)}, bf16[80,1152]{1,0:T(8,128)(2,1)S(1)}, u32[]{:S(2)}, u32[]{:S(2)}) collective-permute-start(bf16[80,1152]{1,0:T(8,128)(2,1)S(1)} %pad_maximum_fusion.4), channel_id=1, source_target_pairs={{0,24},{8,16},{16,8},{24,0},{1,25},{9,17},{17,9},{25,1},{2,26},{10... | collective-permute-start | bytes 552968 | tf_op jit(solution)/shard_map/ppermute | solution.py:93
  106.3 1.9 %collective-permute-start.3 = (bf16[4,2,152,1152]{3,2,1,0:T(8,128)(2,1)S(1)}, bf16[4,2,152,1152]{3,2,1,0:T(8,128)(2,1)S(1)}, u32[]{:S(2)}, u32[]{:S(2)}) collective-permute-start(bf16[4,2,152,1152]{3,2,1,0:T(8,128)(2,1)S(1)} %pad_maximum_fusion), channel_id=1, source_target_pairs={{0,1},{1,0},{2,3},{3,2},{4,5},{5,4},{6,7},{7,6},{8,9},{9,8},{10,11... | collective-permute-start | bytes 8405000 | tf_op jit(solution)/shard_map/ppermute | solution.py:90
  108.2 4.7 %collective-permute-done.18 = bf16[80,1152]{1,0:T(8,128)(2,1)S(1)} collective-permute-done((bf16[80,1152]{1,0:T(8,128)(2,1)S(1)}, bf16[80,1152]{1,0:T(8,128)(2,1)S(1)}, u32[]{:S(2)}, u32[]{:S(2)}) %collective-permute-start.18) | collective-permute-done | bytes 184352 | tf_op jit(solution)/shard_map/ppermute | solution.py:93
  113.4 1.3 collective-permute-start.21
  114.7 2.4 %collective-permute-start.20 = (bf16[72,1152]{1,0:T(8,128)(2,1)S(1)}, bf16[72,1152]{1,0:T(8,128)(2,1)S(1)}, u32[]{:S(2)}, u32[]{:S(2)}) collective-permute-start(bf16[72,1152]{1,0:T(8,128)(2,1)S(1)} %add_convert_fusion.6), channel_id=1, source_target_pairs={{0,64},{32,96},{64,0},{96,32},{1,65},{33,97},{65,1},{97,33},{2,66}... | collective-permute-start | bytes 497672 | tf_op jit(solution)/shard_map/ppermute | solution.py:93
  117.7 4.7 %collective-permute-done.20 = bf16[72,1152]{1,0:T(8,128)(2,1)S(1)} collective-permute-done((bf16[72,1152]{1,0:T(8,128)(2,1)S(1)}, bf16[72,1152]{1,0:T(8,128)(2,1)S(1)}, u32[]{:S(2)}, u32[]{:S(2)}) %collective-permute-start.20) | collective-permute-done | bytes 165920 | tf_op jit(solution)/shard_map/ppermute | solution.py:93
  124.7 3.3 %collective-permute-start.24 = (bf16[40,1408]{1,0:T(8,128)(2,1)S(1)}, bf16[40,1408]{1,0:T(8,128)(2,1)S(1)}, u32[]{:S(2)}, u32[]{:S(2)}) collective-permute-start(bf16[40,1408]{1,0:T(8,128)(2,1)S(1)} %pad_maximum_fusion.18), channel_id=1, source_target_pairs={{0,6},{2,4},{4,2},{6,0},{1,7},{3,5},{5,3},{7,1},{8,14},{10,12},{12... | collective-permute-start | bytes 337928 | tf_op jit(solution)/shard_map/ppermute | solution.py:93
  128.0 1.9 %select_bitcast_fusion = (bf16[4,1,2,152,1152]{4,3,2,0,1:T(8,128)(2,1)S(1)}, bf16[4,1,2,152,1152]{4,3,2,0,1:T(8,128)(2,1)}) fusion(bf16[4,2,152,1152]{3,2,1,0:T(8,128)(2,1)S(1)} %collective-permute-done.3, pred[]{:T(512)S(6)} %eq.86, bf16[1,2,152,1152]{3,2,1,0:T(8,128)(2,1)S(1)} %get-tuple-element.43, bf16[1,2,152,1152]{3,2,1,0:T(8,128)(2,1)S(1)} %get-tuple-element.44, ...), kind=kLoop, calls=%fused_computation.22 | loop fusion | flops 7004160 | bytes 11206657 | tf_op jit(solution)/shard_map/stack | solution.py:116
  130.6 4.6 %collective-permute-done.23 = bf16[40,1408]{1,0:T(8,128)(2,1)S(1)} collective-permute-done((bf16[40,1408]{1,0:T(8,128)(2,1)S(1)}, bf16[40,1408]{1,0:T(8,128)(2,1)S(1)}, u32[]{:S(2)}, u32[]{:S(2)}) %collective-permute-start.23) | collective-permute-done | bytes 112672 | tf_op jit(solution)/shard_map/ppermute | solution.py:93
  135.8 1.2 multiply_reduce_fusion.1
  141.4 1.3 fusion.167
  144.7 2.4 %collective-permute-start.25 = (bf16[32,2176]{1,0:T(8,128)(2,1)S(1)}, bf16[32,2176]{1,0:T(8,128)(2,1)S(1)}, u32[]{:S(2)}, u32[]{:S(2)}) collective-permute-start(bf16[32,2176]{1,0:T(8,128)(2,1)S(1)} %pad_maximum_fusion.17), channel_id=1, source_target_pairs={{0,2},{2,0},{4,6},{6,4},{1,3},{3,1},{5,7},{7,5},{8,10},{10,8},{12,... | collective-permute-start | bytes 417800 | tf_op jit(solution)/shard_map/ppermute | solution.py:93
  148.0 2.5 %collective-permute-done.27 = bf16[32,2176]{1,0:T(8,128)(2,1)S(1)} collective-permute-done((bf16[32,2176]{1,0:T(8,128)(2,1)S(1)}, bf16[32,2176]{1,0:T(8,128)(2,1)S(1)}, u32[]{:S(2)}, u32[]{:S(2)}) %collective-permute-start.27) | collective-permute-done | bytes 139296 | tf_op jit(solution)/shard_map/ppermute | solution.py:93
  151.1 1.2 multiply_reduce_fusion
  157.9 1.6 concatenate.87
  159.5 1.2 convolution_divide_fusion
  160.8 1.4 convolution_divide_fusion.1
  163.0 4.9 %collective-permute-start.28 = (f32[40,2304]{1,0:T(8,128)}, f32[40,2304]{1,0:T(8,128)}, u32[]{:S(2)}, u32[]{:S(2)}) collective-permute-start(f32[40,2304]{1,0:T(8,128)} %select_maximum_fusion), channel_id=1, source_target_pairs={{0,1},{1,0},{2,3},{3,2},{4,5},{5,4},{6,7},{7,6},{8,9},{9,8},{10,11... | collective-permute-start | bytes 1105928 | tf_op jit(solution)/shard_map/ppermute | solution.py:90
  167.8 2.7 %fusion.3 = bf16[2,4,2,144,1152]{4,3,0,1,2:T(8,128)(2,1)S(1)} fusion(bf16[4,1,2,152,1152]{4,3,2,0,1:T(8,128)(2,1)} %get-tuple-element.35, bf16[4,1,2,152,1152]{4,3,2,0,1:T(8,128)(2,1)S(1)} %get-tuple-element.34), kind=kLoop, calls=%fused_computation.11 | loop fusion | flops 2654208 | bytes 10911744 | tf_op jit(solution)/shard_map/transpose | solution.py:119
  170.6 2.8 %copy.14 = bf16[2,4,2,144,1152]{4,3,2,1,0:T(8,128)(2,1)} copy(bf16[2,4,2,144,1152]{4,3,0,1,2:T(8,128)(2,1)S(1)} %fusion.3) | data formatting | bytes 10616832 | tf_op jit(solution)/shard_map/transpose | solution.py:119
  173.6 1.2 broadcast_select_fusion.1
  178.6 2.2 %multiply_add_fusion = (f32[2,144,1152]{2,1,0:T(8,128)}, f32[1,2,144,1152]{3,2,1,0:T(8,128)}) fusion(f32[2,144,1152]{2,1,0:T(8,128)S(1)} %copy-done.4, f32[1,144,1152]{2,1,0:T(8,128)S(1)} %copy-done.2, f32[1,144,1152]{2,1,0:T(8,128)S(1)} %get-tuple-element.51, bf16[2,192,1152]{2,1,0:T(8,128)(2,1)S(1)} %constant_dynamic-update-slice_fusion.5, ...), kind=kOutput, calls=%fused_computation.37 | convolution fusion | flops 129060864 | bytes 6389764 | tf_op jit(solution)/shard_map/lkr,lke->lre/dot_general | solution.py:218
  180.8 4.2 %fusion.1 = bf16[2,1152,1152]{2,1,0:T(8,128)(2,1)} fusion(bf16[2,192,1152]{2,1,0:T(8,128)(2,1)S(1)} %get-tuple-element.87, bf16[2,192,1152]{2,1,0:T(8,128)(2,1)S(1)} %constant_dynamic-update-slice_fusion.5, bf16[2,1152,1152]{2,1,0:T(8,128)(2,1)S(1)} %bitcast.188), kind=kOutput, calls=%fused_computation.3 | convolution fusion | flops 1029832704 | bytes 12386304 | tf_op jit(solution)/shard_map/lkr,lke->lre/dot_general | solution.py:221
  (213 shorter events, 29.0 us)
Async XLA Ops:
  10.8 8.0 %copy-start.5 = (bf16[1152,1152]{1,0:T(8,128)(2,1)}, bf16[1152,1152]{1,0:T(8,128)(2,1)S(1)}, u32[]{:S(2)}) copy-start(bf16[1152,1152]{1,0:T(8,128)(2,1)S(1)} %convolution_convert_fusion.1) | copy-start | bytes 7962628
  12.1 4.4 %collective-permute-start.4 = (bf16[4,144,1152]{2,1,0:T(8,128)(2,1)}, bf16[4,144,1152]{2,1,0:T(8,128)(2,1)}, u32[]{:S(2)}, u32[]{:S(2)}) collective-permute-start(bf16[4,144,1152]{2,1,0:T(8,128)(2,1)} %dynamic-slice_bitcast_fusion.1), channel_id=1, source_target_pairs={{0,1},{1,0},{2,3},{3,2},{4,5},{5,4},{6,7},{7,6},{8,9},{9,8},{10,11... | collective-permute-start | bytes 3981320 | tf_op jit(solution)/shard_map/ppermute | solution.py:90
  18.8 13.3 %slice-start.2 = ((s8[9437184]{0:T(1024)(128)(4,1)}), s8[4194304]{0:T(1024)(128)(4,1)S(1)}, s32[]{:S(2)}) async-start(s8[9437184]{0:T(1024)(128)(4,1)} %bitcast.189), calls=%async_computation.2 | async-start | bytes 8388608
  18.8 13.3 %slice-start.3 = ((s8[9437184]{0:T(1024)(128)(4,1)}), s8[4194304]{0:T(1024)(128)(4,1)S(1)}, s32[]{:S(2)}) async-start(s8[9437184]{0:T(1024)(128)(4,1)} %bitcast.189), calls=%async_computation.3 | async-start | bytes 8388608
  18.8 13.3 %slice-start.4 = ((s8[9437184]{0:T(1024)(128)(4,1)}), s8[1048576]{0:T(1024)(128)(4,1)S(1)}, s32[]{:S(2)}) async-start(s8[9437184]{0:T(1024)(128)(4,1)} %bitcast.189), calls=%async_computation.4 | async-start | bytes 2097152
  31.7 5.8 %collective-permute-start.8 = (bf16[4,144,1152]{2,1,0:T(8,128)(2,1)}, bf16[4,144,1152]{2,1,0:T(8,128)(2,1)S(1)}, u32[]{:S(2)}, u32[]{:S(2)}) collective-permute-start(bf16[4,144,1152]{2,1,0:T(8,128)(2,1)} %dynamic-slice_bitcast_fusion), channel_id=1, source_target_pairs={{0,1},{1,0},{2,3},{3,2},{4,5},{5,4},{6,7},{7,6},{8,9},{9,8},{10,11... | collective-permute-start | bytes 3981320 | tf_op jit(solution)/shard_map/ppermute | solution.py:90
  33.3 3.2 %copy-start.26 = (f32[2,144]{1,0:T(2,128)S(1)}, f32[2,144]{1,0:T(2,128)}, u32[]{:S(2)}) copy-start(f32[2,144]{1,0:T(2,128)} %param.14) | copy-start | bytes 3460
  33.6 18.2 %collective-permute-start.7 = (bf16[144,1152]{1,0:T(8,128)(2,1)}, bf16[144,1152]{1,0:T(8,128)(2,1)S(1)}, u32[]{:S(2)}, u32[]{:S(2)}) collective-permute-start(bf16[144,1152]{1,0:T(8,128)(2,1)} %get-tuple-element.39), channel_id=1, source_target_pairs={{0,6},{2,4},{4,2},{6,0},{1,7},{3,5},{5,3},{7,1},{8,14},{10,12},{12... | collective-permute-start | bytes 995336 | tf_op jit(solution)/shard_map/ppermute | solution.py:93
  36.5 17.6 %collective-permute-start.6 = (bf16[144,1152]{1,0:T(8,128)(2,1)}, bf16[144,1152]{1,0:T(8,128)(2,1)S(1)}, u32[]{:S(2)}, u32[]{:S(2)}) collective-permute-start(bf16[144,1152]{1,0:T(8,128)(2,1)} %get-tuple-element.40), channel_id=1, source_target_pairs={{0,4},{2,6},{4,0},{6,2},{1,5},{3,7},{5,1},{7,3},{8,12},{10,14},{12... | collective-permute-start | bytes 995336 | tf_op jit(solution)/shard_map/ppermute | solution.py:93
  37.0 18.7 %collective-permute-start.5 = (bf16[144,1152]{1,0:T(8,128)(2,1)}, bf16[144,1152]{1,0:T(8,128)(2,1)S(1)}, u32[]{:S(2)}, u32[]{:S(2)}) collective-permute-start(bf16[144,1152]{1,0:T(8,128)(2,1)} %get-tuple-element.41), channel_id=1, source_target_pairs={{0,2},{2,0},{4,6},{6,4},{1,3},{3,1},{5,7},{7,5},{8,10},{10,8},{12,... | collective-permute-start | bytes 995336 | tf_op jit(solution)/shard_map/ppermute | solution.py:93
  37.5 15.7 %copy-start.31 = (bf16[2,144]{1,0:T(2,128)(2,1)S(1)}, bf16[2,144]{1,0:T(2,128)(2,1)}, u32[]{:S(2)}) copy-start(bf16[2,144]{1,0:T(2,128)(2,1)} %param.11) | copy-start | bytes 1732
  39.8 19.9 %collective-permute-start.9 = (bf16[144,1152]{1,0:T(8,128)(2,1)}, bf16[144,1152]{1,0:T(8,128)(2,1)S(1)}, u32[]{:S(2)}, u32[]{:S(2)}) collective-permute-start(bf16[144,1152]{1,0:T(8,128)(2,1)} %get-tuple-element.36), channel_id=1, source_target_pairs={{0,2},{2,0},{4,6},{6,4},{1,3},{3,1},{5,7},{7,5},{8,10},{10,8},{12,... | collective-permute-start | bytes 995336 | tf_op jit(solution)/shard_map/ppermute | solution.py:93
  40.9 21.0 %collective-permute-start.11 = (bf16[144,1152]{1,0:T(8,128)(2,1)}, bf16[144,1152]{1,0:T(8,128)(2,1)}, u32[]{:S(2)}, u32[]{:S(2)}) collective-permute-start(bf16[144,1152]{1,0:T(8,128)(2,1)} %get-tuple-element.37), channel_id=1, source_target_pairs={{0,6},{2,4},{4,2},{6,0},{1,7},{3,5},{5,3},{7,1},{8,14},{10,12},{12... | collective-permute-start | bytes 995336 | tf_op jit(solution)/shard_map/ppermute | solution.py:93
  51.8 10.1 %copy-start.10 = (bf16[144,1152]{1,0:T(8,128)(2,1)}, bf16[144,1152]{1,0:T(8,128)(2,1)S(1)}, u32[]{:S(2)}) copy-start(bf16[144,1152]{1,0:T(8,128)(2,1)S(1)} %collective-permute-done.7) | copy-start | bytes 995332
  51.8 16.9 %collective-permute-start.10 = (bf16[144,1152]{1,0:T(8,128)(2,1)}, bf16[144,1152]{1,0:T(8,128)(2,1)}, u32[]{:S(2)}, u32[]{:S(2)}) collective-permute-start(bf16[144,1152]{1,0:T(8,128)(2,1)} %get-tuple-element.38), channel_id=1, source_target_pairs={{0,4},{2,6},{4,0},{6,2},{1,5},{3,7},{5,1},{7,3},{8,12},{10,14},{12... | collective-permute-start | bytes 995336 | tf_op jit(solution)/shard_map/ppermute | solution.py:93
  54.1 7.7 %copy-start.11 = (bf16[144,1152]{1,0:T(8,128)(2,1)}, bf16[144,1152]{1,0:T(8,128)(2,1)S(1)}, u32[]{:S(2)}) copy-start(bf16[144,1152]{1,0:T(8,128)(2,1)S(1)} %collective-permute-done.6) | copy-start | bytes 995332
  54.1 27.8 %collective-permute-start.2 = (bf16[2,152,1152]{2,1,0:T(8,128)(2,1)}, bf16[2,152,1152]{2,1,0:T(8,128)(2,1)}, u32[]{:S(2)}, u32[]{:S(2)}) collective-permute-start(bf16[2,152,1152]{2,1,0:T(8,128)(2,1)} %fusion.25), channel_id=1, source_target_pairs={{0,2},{2,0},{4,6},{6,4},{1,3},{3,1},{5,7},{7,5},{8,10},{10,8},{12,... | collective-permute-start | bytes 2101256 | tf_op jit(solution)/shard_map/ppermute | solution.py:93
  55.8 6.1 %copy-start.12 = (bf16[144,1152]{1,0:T(8,128)(2,1)}, bf16[144,1152]{1,0:T(8,128)(2,1)S(1)}, u32[]{:S(2)}) copy-start(bf16[144,1152]{1,0:T(8,128)(2,1)S(1)} %collective-permute-done.5) | copy-start | bytes 995332
  55.8 42.9 %collective-permute-start.1 = (bf16[2,152,1152]{2,1,0:T(8,128)(2,1)}, bf16[2,152,1152]{2,1,0:T(8,128)(2,1)}, u32[]{:S(2)}, u32[]{:S(2)}) collective-permute-start(bf16[2,152,1152]{2,1,0:T(8,128)(2,1)} %fusion.25), channel_id=1, source_target_pairs={{0,4},{2,6},{4,0},{6,2},{1,5},{3,7},{5,1},{7,3},{8,12},{10,14},{12... | collective-permute-start | bytes 2101256 | tf_op jit(solution)/shard_map/ppermute | solution.py:93
  59.7 39.0 %collective-permute-start = (bf16[2,152,1152]{2,1,0:T(8,128)(2,1)}, bf16[2,152,1152]{2,1,0:T(8,128)(2,1)}, u32[]{:S(2)}, u32[]{:S(2)}) collective-permute-start(bf16[2,152,1152]{2,1,0:T(8,128)(2,1)} %fusion.25), channel_id=1, source_target_pairs={{0,6},{2,4},{4,2},{6,0},{1,7},{3,5},{5,3},{7,1},{8,14},{10,12},{12... | collective-permute-start | bytes 2101256 | tf_op jit(solution)/shard_map/ppermute | solution.py:93
  71.6 3.5 %collective-permute-start.12 = (bf16[152,1152]{1,0:T(8,128)(2,1)S(1)}, bf16[152,1152]{1,0:T(8,128)(2,1)S(1)}, u32[]{:S(2)}, u32[]{:S(2)}) collective-permute-start(bf16[152,1152]{1,0:T(8,128)(2,1)S(1)} %pad_maximum_fusion.8), channel_id=1, source_target_pairs={{0,1},{1,0},{2,3},{3,2},{4,5},{5,4},{6,7},{7,6},{8,9},{9,8},{10,11... | collective-permute-start | bytes 1050632 | tf_op jit(solution)/shard_map/ppermute | solution.py:90
  75.4 25.7 %collective-permute-start.13 = (bf16[80,1152]{1,0:T(8,128)(2,1)S(1)}, bf16[80,1152]{1,0:T(8,128)(2,1)S(1)}, u32[]{:S(2)}, u32[]{:S(2)}) collective-permute-start(bf16[80,1152]{1,0:T(8,128)(2,1)S(1)} %get-tuple-element.82), channel_id=1, source_target_pairs={{0,32},{32,0},{64,96},{96,64},{1,33},{33,1},{65,97},{97,65},{2,34}... | collective-permute-start | bytes 552968 | tf_op jit(solution)/shard_map/ppermute | solution.py:93
  76.7 24.4 %collective-permute-start.14 = (bf16[80,1152]{1,0:T(8,128)(2,1)S(1)}, bf16[80,1152]{1,0:T(8,128)(2,1)S(1)}, u32[]{:S(2)}, u32[]{:S(2)}) collective-permute-start(bf16[80,1152]{1,0:T(8,128)(2,1)S(1)} %get-tuple-element.83), channel_id=1, source_target_pairs={{0,64},{32,96},{64,0},{96,32},{1,65},{33,97},{65,1},{97,33},{2,66}... | collective-permute-start | bytes 552968 | tf_op jit(solution)/shard_map/ppermute | solution.py:93
  82.0 19.2 %collective-permute-start.15 = (bf16[80,1152]{1,0:T(8,128)(2,1)S(1)}, bf16[80,1152]{1,0:T(8,128)(2,1)S(1)}, u32[]{:S(2)}, u32[]{:S(2)}) collective-permute-start(bf16[80,1152]{1,0:T(8,128)(2,1)S(1)} %get-tuple-element.84), channel_id=1, source_target_pairs={{0,96},{32,64},{64,32},{96,0},{1,97},{33,65},{65,33},{97,1},{2,98}... | collective-permute-start | bytes 552968 | tf_op jit(solution)/shard_map/ppermute | solution.py:93
  101.3 11.6 %collective-permute-start.18 = (bf16[80,1152]{1,0:T(8,128)(2,1)S(1)}, bf16[80,1152]{1,0:T(8,128)(2,1)S(1)}, u32[]{:S(2)}, u32[]{:S(2)}) collective-permute-start(bf16[80,1152]{1,0:T(8,128)(2,1)S(1)} %pad_maximum_fusion.4), channel_id=1, source_target_pairs={{0,24},{8,16},{16,8},{24,0},{1,25},{9,17},{17,9},{25,1},{2,26},{10... | collective-permute-start | bytes 552968 | tf_op jit(solution)/shard_map/ppermute | solution.py:93
  105.2 7.8 %collective-permute-start.17 = (bf16[80,1152]{1,0:T(8,128)(2,1)S(1)}, bf16[80,1152]{1,0:T(8,128)(2,1)S(1)}, u32[]{:S(2)}, u32[]{:S(2)}) collective-permute-start(bf16[80,1152]{1,0:T(8,128)(2,1)S(1)} %pad_maximum_fusion.4), channel_id=1, source_target_pairs={{0,16},{8,24},{16,0},{24,8},{1,17},{9,25},{17,1},{25,9},{2,18},{10... | collective-permute-start | bytes 552968 | tf_op jit(solution)/shard_map/ppermute | solution.py:93
  105.2 8.2 %collective-permute-start.16 = (bf16[80,1152]{1,0:T(8,128)(2,1)S(1)}, bf16[80,1152]{1,0:T(8,128)(2,1)S(1)}, u32[]{:S(2)}, u32[]{:S(2)}) collective-permute-start(bf16[80,1152]{1,0:T(8,128)(2,1)S(1)} %pad_maximum_fusion.4), channel_id=1, source_target_pairs={{0,8},{8,0},{16,24},{24,16},{1,9},{9,1},{17,25},{25,17},{2,10},{10... | collective-permute-start | bytes 552968 | tf_op jit(solution)/shard_map/ppermute | solution.py:93
  106.3 21.7 %collective-permute-start.3 = (bf16[4,2,152,1152]{3,2,1,0:T(8,128)(2,1)S(1)}, bf16[4,2,152,1152]{3,2,1,0:T(8,128)(2,1)S(1)}, u32[]{:S(2)}, u32[]{:S(2)}) collective-permute-start(bf16[4,2,152,1152]{3,2,1,0:T(8,128)(2,1)S(1)} %pad_maximum_fusion), channel_id=1, source_target_pairs={{0,1},{1,0},{2,3},{3,2},{4,5},{5,4},{6,7},{7,6},{8,9},{9,8},{10,11... | collective-permute-start | bytes 8405000 | tf_op jit(solution)/shard_map/ppermute | solution.py:90
  113.4 4.3 %collective-permute-start.21 = (bf16[72,1152]{1,0:T(8,128)(2,1)S(1)}, bf16[72,1152]{1,0:T(8,128)(2,1)S(1)}, u32[]{:S(2)}, u32[]{:S(2)}) collective-permute-start(bf16[72,1152]{1,0:T(8,128)(2,1)S(1)} %add_convert_fusion.6), channel_id=1, source_target_pairs={{0,32},{32,0},{64,96},{96,64},{1,33},{33,1},{65,97},{97,65},{2,34}... | collective-permute-start | bytes 497672 | tf_op jit(solution)/shard_map/ppermute | solution.py:93
  114.7 7.7 %collective-permute-start.20 = (bf16[72,1152]{1,0:T(8,128)(2,1)S(1)}, bf16[72,1152]{1,0:T(8,128)(2,1)S(1)}, u32[]{:S(2)}, u32[]{:S(2)}) collective-permute-start(bf16[72,1152]{1,0:T(8,128)(2,1)S(1)} %add_convert_fusion.6), channel_id=1, source_target_pairs={{0,64},{32,96},{64,0},{96,32},{1,65},{33,97},{65,1},{97,33},{2,66}... | collective-permute-start | bytes 497672 | tf_op jit(solution)/shard_map/ppermute | solution.py:93
  117.2 6.3 %collective-permute-start.19 = (bf16[72,1152]{1,0:T(8,128)(2,1)S(1)}, bf16[72,1152]{1,0:T(8,128)(2,1)S(1)}, u32[]{:S(2)}, u32[]{:S(2)}) collective-permute-start(bf16[72,1152]{1,0:T(8,128)(2,1)S(1)} %add_convert_fusion.6), channel_id=1, source_target_pairs={{0,96},{32,64},{64,32},{96,0},{1,97},{33,65},{65,33},{97,1},{2,98}... | collective-permute-start | bytes 497672 | tf_op jit(solution)/shard_map/ppermute | solution.py:93
  124.7 5.9 %collective-permute-start.24 = (bf16[40,1408]{1,0:T(8,128)(2,1)S(1)}, bf16[40,1408]{1,0:T(8,128)(2,1)S(1)}, u32[]{:S(2)}, u32[]{:S(2)}) collective-permute-start(bf16[40,1408]{1,0:T(8,128)(2,1)S(1)} %pad_maximum_fusion.18), channel_id=1, source_target_pairs={{0,6},{2,4},{4,2},{6,0},{1,7},{3,5},{5,3},{7,1},{8,14},{10,12},{12... | collective-permute-start | bytes 337928 | tf_op jit(solution)/shard_map/ppermute | solution.py:93
  129.9 5.2 %collective-permute-start.23 = (bf16[40,1408]{1,0:T(8,128)(2,1)S(1)}, bf16[40,1408]{1,0:T(8,128)(2,1)S(1)}, u32[]{:S(2)}, u32[]{:S(2)}) collective-permute-start(bf16[40,1408]{1,0:T(8,128)(2,1)S(1)} %pad_maximum_fusion.18), channel_id=1, source_target_pairs={{0,4},{2,6},{4,0},{6,2},{1,5},{3,7},{5,1},{7,3},{8,12},{10,14},{12... | collective-permute-start | bytes 337928 | tf_op jit(solution)/shard_map/ppermute | solution.py:93
  129.9 5.9 %collective-permute-start.22 = (bf16[40,1408]{1,0:T(8,128)(2,1)S(1)}, bf16[40,1408]{1,0:T(8,128)(2,1)S(1)}, u32[]{:S(2)}, u32[]{:S(2)}) collective-permute-start(bf16[40,1408]{1,0:T(8,128)(2,1)S(1)} %pad_maximum_fusion.18), channel_id=1, source_target_pairs={{0,2},{2,0},{4,6},{6,4},{1,3},{3,1},{5,7},{7,5},{8,10},{10,8},{12,... | collective-permute-start | bytes 337928 | tf_op jit(solution)/shard_map/ppermute | solution.py:93
  130.6 6.5 %copy-start.28 = (bf16[40,1408]{1,0:T(8,128)(2,1)}, bf16[40,1408]{1,0:T(8,128)(2,1)S(1)}, u32[]{:S(2)}) copy-start(bf16[40,1408]{1,0:T(8,128)(2,1)S(1)} %collective-permute-done.24) | copy-start | bytes 337924
  137.8 5.0 %copy-start.16 = (bf16[72,1152]{1,0:T(8,128)(2,1)S(1)}, bf16[72,1152]{1,0:T(8,128)(2,1)}, u32[]{:S(2)}) copy-start(bf16[72,1152]{1,0:T(8,128)(2,1)} %copy-done.15) | copy-start | bytes 497668
  137.8 5.0 %copy-start.18 = (bf16[72,1152]{1,0:T(8,128)(2,1)S(1)}, bf16[72,1152]{1,0:T(8,128)(2,1)}, u32[]{:S(2)}) copy-start(bf16[72,1152]{1,0:T(8,128)(2,1)} %copy-done.17) | copy-start | bytes 497668
  137.8 5.0 %copy-start.20 = (bf16[72,1152]{1,0:T(8,128)(2,1)S(1)}, bf16[72,1152]{1,0:T(8,128)(2,1)}, u32[]{:S(2)}) copy-start(bf16[72,1152]{1,0:T(8,128)(2,1)} %copy-done.19) | copy-start | bytes 497668
  137.8 5.0 %copy-start.22 = (bf16[72,1152]{1,0:T(8,128)(2,1)S(1)}, bf16[72,1152]{1,0:T(8,128)(2,1)}, u32[]{:S(2)}) copy-start(bf16[72,1152]{1,0:T(8,128)(2,1)} %copy-done.21) | copy-start | bytes 497668
  143.8 6.7 %collective-permute-start.27 = (bf16[32,2176]{1,0:T(8,128)(2,1)S(1)}, bf16[32,2176]{1,0:T(8,128)(2,1)S(1)}, u32[]{:S(2)}, u32[]{:S(2)}) collective-permute-start(bf16[32,2176]{1,0:T(8,128)(2,1)S(1)} %pad_maximum_fusion.17), channel_id=1, source_target_pairs={{0,6},{2,4},{4,2},{6,0},{1,7},{3,5},{5,3},{7,1},{8,14},{10,12},{12... | collective-permute-start | bytes 417800 | tf_op jit(solution)/shard_map/ppermute | solution.py:93
  144.7 5.8 %collective-permute-start.26 = (bf16[32,2176]{1,0:T(8,128)(2,1)S(1)}, bf16[32,2176]{1,0:T(8,128)(2,1)S(1)}, u32[]{:S(2)}, u32[]{:S(2)}) collective-permute-start(bf16[32,2176]{1,0:T(8,128)(2,1)S(1)} %pad_maximum_fusion.17), channel_id=1, source_target_pairs={{0,4},{2,6},{4,0},{6,2},{1,5},{3,7},{5,1},{7,3},{8,12},{10,14},{12... | collective-permute-start | bytes 417800 | tf_op jit(solution)/shard_map/ppermute | solution.py:93
  144.7 6.4 %collective-permute-start.25 = (bf16[32,2176]{1,0:T(8,128)(2,1)S(1)}, bf16[32,2176]{1,0:T(8,128)(2,1)S(1)}, u32[]{:S(2)}, u32[]{:S(2)}) collective-permute-start(bf16[32,2176]{1,0:T(8,128)(2,1)S(1)} %pad_maximum_fusion.17), channel_id=1, source_target_pairs={{0,2},{2,0},{4,6},{6,4},{1,3},{3,1},{5,7},{7,5},{8,10},{10,8},{12,... | collective-permute-start | bytes 417800 | tf_op jit(solution)/shard_map/ppermute | solution.py:93
  160.8 7.0 %copy-start.8 = (f32[32,1152]{1,0:T(8,128)}, f32[32,1152]{1,0:T(8,128)S(1)}, u32[]{:S(2)}) copy-start(f32[32,1152]{1,0:T(8,128)S(1)} %convolution_divide_fusion) | copy-start | bytes 442372
  162.2 5.6 %copy-start.9 = (f32[32,1152]{1,0:T(8,128)}, f32[32,1152]{1,0:T(8,128)S(1)}, u32[]{:S(2)}) copy-start(f32[32,1152]{1,0:T(8,128)S(1)} %convolution_divide_fusion.1) | copy-start | bytes 442372
  163.0 10.6 %collective-permute-start.28 = (f32[40,2304]{1,0:T(8,128)}, f32[40,2304]{1,0:T(8,128)}, u32[]{:S(2)}, u32[]{:S(2)}) collective-permute-start(f32[40,2304]{1,0:T(8,128)} %select_maximum_fusion), channel_id=1, source_target_pairs={{0,1},{1,0},{2,3},{3,2},{4,5},{5,4},{6,7},{7,6},{8,9},{9,8},{10,11... | collective-permute-start | bytes 1105928 | tf_op jit(solution)/shard_map/ppermute | solution.py:90
  170.6 2.8 %copy-start = (bf16[4,1,2,152,1152]{4,3,2,0,1:T(8,128)(2,1)S(1)}, bf16[4,1,2,152,1152]{4,3,2,0,1:T(8,128)(2,1)}, u32[]{:S(2)}) copy-start(bf16[4,1,2,152,1152]{4,3,2,0,1:T(8,128)(2,1)} %get-tuple-element.35) | copy-start | bytes 8404996
  173.5 7.2 %slice-start = ((s8[5308416]{0:T(1024)(128)(4,1)}), s8[1114112]{0:T(1024)(128)(4,1)S(1)}, s32[]{:S(2)}) async-start(s8[5308416]{0:T(1024)(128)(4,1)} %bitcast.186), calls=%async_computation | async-start | bytes 2228224
  176.7 4.1 %slice-start.1 = ((s8[5308416]{0:T(1024)(128)(4,1)}), s8[4194304]{0:T(1024)(128)(4,1)S(1)}, s32[]{:S(2)}) async-start(s8[5308416]{0:T(1024)(128)(4,1)} %bitcast.186), calls=%async_computation.1 | async-start | bytes 8388608
  (18 other events, 28.3 us)
